TPU v7x, 128 devices: a whole 4x4x4 slice. The times are simulated.
128 devices in a mesh: dp: 8 (over z, core), expert: 16 (over y, x).
Axes of the slice: x: 4, y: 4, z: 4, core: 2. Of those that a mesh axis runs over, the one named last changes fastest.
Arguments:
- tokens: bfloat16 [16384, 4096], P(('dp', 'expert')), may hold values from -24 to 24
- cotangent: bfloat16 [16384, 4096], P(('dp', 'expert')), may hold values from -6 to 6
- expert_ids: int32 [16384, 8], P(('dp', 'expert')), may hold values from 0 to 15, all different within a row; in each aligned block of 128 rows (0 to 127, 128 to 255, ...) at most 72 rows name the same one
- route_weight: float32 [16384, 8], P(('dp', 'expert')), may hold values from 0.02 to 0.5
- up_weight: bfloat16 [16, 4096, 768], P('expert'), may hold values from -0.09375 to 0.09375
- down_weight: bfloat16 [16, 768, 4096], P('expert'), may hold values from -0.21875 to 0.21875
Outputs:
- token_grad: bfloat16 [16384, 4096], P(('dp', 'expert'))
- up_grad: float32 [16, 4096, 768], P('expert', 'dp')
- down_grad: float32 [16, 768, 4096], P('expert', 'dp')
Inputs may be any that keep to these rules, and one draw needn't show every extreme that they name: `expert_ids`: each row names 8 different experts. Among the 128 tokens of one device (aligned blocks) no expert is named more than 72 times, a bound that some block reaches.
All inputs are finite; a program needn't handle non-finite values.
Results may differ from a plain program's by a relative error of at most 0.017.
Values may be sent and summed in bfloat16 or wider, within the bound.
No kernel may reach another device: no remote copies, remote signals or barrier semaphores. Data moves between devices by JAX's collectives and lax.ppermute only.
A program may use at most 192 MiB of HBM per device.

v0:
```python
import jax
import jax.numpy as jnp
from jax import lax
from jax.sharding import PartitionSpec as P


def expert_math(rows_x, rows_g, up_matrix, down_matrix):
    pre = jnp.dot(rows_x, up_matrix, preferred_element_type=jnp.float32)
    sigma = jax.nn.sigmoid(pre)
    active = (pre * sigma).astype(jnp.bfloat16)
    back = lax.dot_general(
        rows_g, down_matrix, (((1,), (1,)), ((), ())), preferred_element_type=jnp.float32
    )
    pre_grad = (back * sigma * (1.0 + pre * (1.0 - sigma))).astype(jnp.bfloat16)
    row_grad = lax.dot_general(
        pre_grad, up_matrix, (((1,), (1,)), ((), ())), preferred_element_type=jnp.float32
    ).astype(jnp.bfloat16)
    return (active, pre_grad, row_grad)


def body(tokens, cotangent, expert_ids, route_weight, up_weight, down_weight):
    groups = lax.axis_size("expert")
    tok_rows, width = tokens.shape
    top_count = expert_ids.shape[1]
    capacity = tok_rows * top_count * 9 // (8 * groups)
    up_matrix = up_weight[0]
    down_matrix = down_weight[0]
    flat_ids = expert_ids.reshape(-1)
    onehot = (flat_ids[:, None] == jnp.arange(groups, dtype=jnp.int32)[None, :]).astype(jnp.int32)
    earlier = jnp.cumsum(onehot, axis=0) - onehot
    slot_of = jnp.sum(earlier * onehot, axis=1)
    target = flat_ids * capacity + slot_of
    token_of = jnp.arange(tok_rows * top_count, dtype=jnp.int32) // top_count
    scaled = (route_weight[:, :, None] * cotangent[:, None, :].astype(jnp.float32)).astype(
        jnp.bfloat16
    )
    scaled = scaled.reshape(tok_rows * top_count, width)
    send_x = jnp.zeros((groups * capacity, width), jnp.bfloat16).at[target].set(tokens[token_of])
    send_g = jnp.zeros((groups * capacity, width), jnp.bfloat16).at[target].set(scaled)
    send_x = send_x.reshape(groups, capacity, width)
    send_g = send_g.reshape(groups, capacity, width)
    recv_x, recv_g = (
        lax.all_to_all(send_x, "expert", split_axis=0, concat_axis=0, tiled=True),
        lax.all_to_all(send_g, "expert", split_axis=0, concat_axis=0, tiled=True),
    )
    flat_x = recv_x.reshape(-1, width)
    flat_g = recv_g.reshape(-1, width)
    active, pre_grad, row_grad = expert_math(flat_x, flat_g, up_matrix, down_matrix)
    returned = lax.all_to_all(
        row_grad.reshape(groups, capacity, width), "expert", split_axis=0, concat_axis=0, tiled=True
    )
    picked = returned.reshape(-1, width)[target]
    token_grad = jnp.sum(
        picked.reshape(tok_rows, top_count, width).astype(jnp.float32), axis=1
    ).astype(jnp.bfloat16)
    columns = flat_x
    up_grad = lax.psum_scatter(
        lax.dot_general(
            columns, pre_grad, (((0,), (0,)), ((), ())), preferred_element_type=jnp.float32
        ).astype(jnp.bfloat16),
        "dp",
        scatter_dimension=0,
        tiled=True,
    ).astype(jnp.float32)
    columns = active
    down_grad = lax.psum_scatter(
        lax.dot_general(
            columns, flat_g, (((0,), (0,)), ((), ())), preferred_element_type=jnp.float32
        ).astype(jnp.bfloat16),
        "dp",
        scatter_dimension=0,
        tiled=True,
    ).astype(jnp.float32)
    return (token_grad, up_grad[None], down_grad[None])


def solution(mesh):
    in_specs = (
        P(("dp", "expert"), None),
        P(("dp", "expert"), None),
        P(("dp", "expert"), None),
        P(("dp", "expert"), None),
        P("expert", None, None),
        P("expert", None, None),
    )
    out_specs = (P(("dp", "expert"), None), P("expert", "dp", None), P("expert", "dp", None))
    return jax.shard_map(body, mesh=mesh, in_specs=in_specs, out_specs=out_specs, check_vma=False)
```

profile of v0, /device:TPU:0, one launch (start us, length us, event | category | flops | bytes accessed | tf_op | source)
XLA Modules:
  0.0 566.2 jit_solution(12322814581133346556)
XLA Ops:
  7.2 0.9 copy.12
  8.2 0.7 broadcast_multiply_fusion
  9.0 4.5 reduce-window.6
  14.2 7.7 %gather_fusion = bf16[1024,4096]{1,0:T(8,128)(2,1)} fusion(bf16[128,4096]{1,0:T(8,128)(2,1)S(1)} %copy-done, s32[1024]{0:T(1024)S(1)} %broadcast_clamp_fusion.1), kind=kCustom, calls=%fused_computation | custom fusion | bytes 16781312 | tf_op jit(solution)/shard_map/gather | solution.py:38
  21.9 18.2 %scatter_custom_fusion.1 = bf16[1152,4096]{1,0:T(8,128)(2,1)} fusion(s32[1024]{0:T(1024)S(1)} %bitcast.66, bf16[1024,4096]{1,0:T(8,128)(2,1)} %gather_fusion, bf16[]{:T(256)} %constant.26.clone.1), kind=kCustom, calls=%fused_computation.16 | custom fusion | bytes 9437696 | tf_op jit(solution)/shard_map/scatter | solution.py:38
  40.1 7.5 %all-to-all-start.1 = ((bf16[16,72,4096]{2,1,0:T(8,128)(2,1)}), bf16[16,72,4096]{2,1,0:T(8,128)(2,1)}, u32[]{:S(2)}, u32[]{:S(2)}) async-start(bf16[16,72,4096]{2,1,0:T(8,128)(2,1)} %bitcast.60), calls=%async_computation.1 | async-start | bytes 18874368 | tf_op jit(solution)/shard_map/all_to_all | solution.py:43
  47.8 6.9 %mul.54 = f32[1024,4096]{1,0:T(8,128)} broadcast(f32[1024]{0:T(1024)S(1)} %mul.53), dimensions={0} | broadcast | bytes 16781312 | tf_op jit(solution)/shard_map/mul | solution.py:34
  54.7 7.8 %mul.55 = f32[128,8,4096]{2,1,0:T(8,128)} broadcast(bf16[128,4096]{1,0:T(8,128)(2,1)S(1)} %copy-done.2), dimensions={0,2} | broadcast | bytes 17825792 | tf_op jit(solution)/shard_map/mul | solution.py:34
  62.5 22.6 %scatter_custom_fusion = bf16[1152,4096]{1,0:T(8,128)(2,1)} fusion(s32[1024]{0:T(1024)S(1)} %bitcast.67, f32[1024,4096]{1,0:T(8,128)} %mul.54, f32[128,8,4096]{2,1,0:T(8,128)} %mul.55, bf16[]{:T(256)} %constant.26.clone.1), kind=kCustom, calls=%fused_computation.7 | custom fusion | flops 8388608 | bytes 42991616 | tf_op jit(solution)/shard_map/scatter | solution.py:39
  85.1 102.0 %all-to-all-done.1 = bf16[16,72,4096]{2,1,0:T(8,128)(2,1)} async-done(((bf16[16,72,4096]{2,1,0:T(8,128)(2,1)}), bf16[16,72,4096]{2,1,0:T(8,128)(2,1)}, u32[]{:S(2)}, u32[]{:S(2)}) %all-to-all-start.1) | async-done | bytes 9437216 | tf_op jit(solution)/shard_map/all_to_all | solution.py:43
  187.2 5.7 all-to-all-start
  192.9 13.1 %fusion.4 = f32[1152,768]{1,0:T(8,128)} fusion(bf16[1152,4096]{1,0:T(8,128)(2,1)} %bitcast.10, bf16[1,4096,768]{2,1,0:T(8,128)(2,1)} %param.10), kind=kOutput, calls=%fused_computation.12 | convolution fusion | flops 7247757312 | bytes 19267584 | tf_op jit(solution)/shard_map/dot_general | solution.py:8
  206.0 123.7 %all-to-all-done = bf16[16,72,4096]{2,1,0:T(8,128)(2,1)} async-done(((bf16[16,72,4096]{2,1,0:T(8,128)(2,1)}), bf16[16,72,4096]{2,1,0:T(8,128)(2,1)}, u32[]{:S(2)}, u32[]{:S(2)}) %all-to-all-start) | async-done | bytes 9437216 | tf_op jit(solution)/shard_map/all_to_all | solution.py:44
  329.7 13.0 %fusion.17 = bf16[1152,768]{1,0:T(8,128)(2,1)S(1)} fusion(f32[1152,768]{1,0:T(8,128)} %fusion.4, bf16[1152,4096]{1,0:T(8,128)(2,1)} %bitcast.6, bf16[1,768,4096]{2,1,0:T(8,128)(2,1)} %param.11), kind=kOutput, calls=%fused_computation.23 | convolution fusion | flops 7255719936 | bytes 21037056 | tf_op jit(solution)/shard_map/dot_general | solution.py:11
  342.8 14.2 %convolution_convert_fusion.2 = bf16[4096,768]{1,0:T(8,128)(2,1)} fusion(bf16[1152,4096]{1,0:T(8,128)(2,1)} %bitcast.10, bf16[1152,768]{1,0:T(8,128)(2,1)S(1)} %fusion.17), kind=kOutput, calls=%fused_computation.10 | convolution fusion | flops 7250903040 | bytes 17498112 | tf_op jit(solution)/shard_map/dot_general | solution.py:58
  357.0 0.4 reduce-scatter.5.cloned.1.call-start
  357.5 13.8 %convolution_convert_fusion.1 = bf16[768,4096]{1,0:T(8,128)(2,1)} fusion(bf16[1152,4096]{1,0:T(8,128)(2,1)} %bitcast.6, f32[1152,768]{1,0:T(8,128)} %fusion.4), kind=kOutput, calls=%fused_computation.9 | convolution fusion | flops 7255326720 | bytes 19267584 | tf_op jit(solution)/shard_map/dot_general | solution.py:67
  371.3 12.5 %convolution_convert_fusion = bf16[1152,4096]{1,0:T(8,128)(2,1)} fusion(bf16[1152,768]{1,0:T(8,128)(2,1)S(1)} %fusion.17, bf16[1,4096,768]{2,1,0:T(8,128)(2,1)} %param.10), kind=kOutput, calls=%fused_computation.6 | convolution fusion | flops 7252475904 | bytes 17498112 | tf_op jit(solution)/shard_map/dot_general | solution.py:15
  383.9 5.7 %all-to-all-start.2 = ((bf16[16,72,4096]{2,1,0:T(8,128)(2,1)}), bf16[16,72,4096]{2,1,0:T(8,128)(2,1)}, u32[]{:S(2)}, u32[]{:S(2)}) async-start(bf16[16,72,4096]{2,1,0:T(8,128)(2,1)} %bitcast.62), calls=%async_computation.2 | async-start | bytes 18874368 | tf_op jit(solution)/shard_map/all_to_all | solution.py:49
  389.5 134.7 %all-to-all-done.2 = bf16[16,72,4096]{2,1,0:T(8,128)(2,1)} async-done(((bf16[16,72,4096]{2,1,0:T(8,128)(2,1)}), bf16[16,72,4096]{2,1,0:T(8,128)(2,1)}, u32[]{:S(2)}, u32[]{:S(2)}) %all-to-all-start.2) | async-done | bytes 9437216 | tf_op jit(solution)/shard_map/all_to_all | solution.py:49
  524.2 20.1 %gather_fusion.1 = bf16[1024,4096]{1,0:T(8,128)(2,1)} fusion(bf16[1152,4096]{1,0:T(8,128)(2,1)} %bitcast.13, s32[1024]{0:T(1024)S(1)} %broadcast_clamp_fusion), kind=kCustom, calls=%fused_computation.1 | custom fusion | bytes 16781312 | tf_op jit(solution)/shard_map/gather | solution.py:52
  544.3 10.1 %bitcast_reduce_fusion = bf16[128,4096]{1,0:T(8,128)(2,1)} fusion(bf16[1024,4096]{1,0:T(8,128)(2,1)} %gather_fusion.1), kind=kLoop, calls=%fused_computation.8 | loop fusion | flops 3670016 | bytes 9437184 | tf_op jit(solution)/shard_map/reduce_sum | solution.py:53
  554.4 2.4 bitcast_convert_fusion.1
  556.8 2.4 bitcast_convert_fusion
  (31 shorter events, 1.1 us)
Async XLA Ops:
  7.2 7.0 %copy-start = (bf16[128,4096]{1,0:T(8,128)(2,1)S(1)}, bf16[128,4096]{1,0:T(8,128)(2,1)}, u32[]{:S(2)}) copy-start(bf16[128,4096]{1,0:T(8,128)(2,1)} %param.6) | copy-start | bytes 3145732
  40.1 7.5 %copy-start.3 = (f32[128,8]{0,1:T(8,128)S(1)}, f32[128,8]{0,1:T(8,128)}, u32[]{:S(2)}) copy-start(f32[128,8]{0,1:T(8,128)} %param.9) | copy-start | bytes 12292
  40.1 147.0 %all-to-all-start.1 = ((bf16[16,72,4096]{2,1,0:T(8,128)(2,1)}), bf16[16,72,4096]{2,1,0:T(8,128)(2,1)}, u32[]{:S(2)}, u32[]{:S(2)}) async-start(bf16[16,72,4096]{2,1,0:T(8,128)(2,1)} %bitcast.60), calls=%async_computation.1 | async-start | bytes 18874368 | tf_op jit(solution)/shard_map/all_to_all | solution.py:43
  47.8 6.9 %copy-start.2 = (bf16[128,4096]{1,0:T(8,128)(2,1)S(1)}, bf16[128,4096]{1,0:T(8,128)(2,1)}, u32[]{:S(2)}) copy-start(bf16[128,4096]{1,0:T(8,128)(2,1)} %param.7) | copy-start | bytes 3145732
  187.2 142.6 %all-to-all-start = ((bf16[16,72,4096]{2,1,0:T(8,128)(2,1)}), bf16[16,72,4096]{2,1,0:T(8,128)(2,1)}, u32[]{:S(2)}, u32[]{:S(2)}) async-start(bf16[16,72,4096]{2,1,0:T(8,128)(2,1)} %bitcast.61), calls=%async_computation | async-start | bytes 18874368 | tf_op jit(solution)/shard_map/all_to_all | solution.py:44
  192.8 361.5 %reduce-scatter.3.cloned.1.call-start = ((), (), s32[]{:S(2)}) async-start(), calls=%async_computation.5 | async-start | bytes 7077888 | tf_op jit(solution)/shard_map/reduce_scatter | solution.py:57
  357.0 199.8 %reduce-scatter.5.cloned.1.call-start = ((), (), s32[]{:S(2)}) async-start(), calls=%async_computation.6 | async-start | bytes 7077888 | tf_op jit(solution)/shard_map/reduce_scatter | solution.py:66
  383.9 140.3 %all-to-all-start.2 = ((bf16[16,72,4096]{2,1,0:T(8,128)(2,1)}), bf16[16,72,4096]{2,1,0:T(8,128)(2,1)}, u32[]{:S(2)}, u32[]{:S(2)}) async-start(bf16[16,72,4096]{2,1,0:T(8,128)(2,1)} %bitcast.62), calls=%async_computation.2 | async-start | bytes 18874368 | tf_op jit(solution)/shard_map/all_to_all | solution.py:49
  524.2 35.0 %copy-start.1 = (bf16[128,4096]{1,0:T(8,128)(2,1)S(1)}, bf16[128,4096]{1,0:T(8,128)(2,1)}, u32[]{:S(2)}) copy-start(bf16[128,4096]{1,0:T(8,128)(2,1)} %param.6) | copy-start | bytes 3145732
Sparse Core Ops, SparseCore 0:
  357.1 43.5 reduce-scatter.2
  403.1 43.1 reduce-scatter.4
where the time goes:
time: 575 us; the launch traced here: 566 us
  waiting for transfers between devices  360 us (63%)
  matrix products  66.7 us (12%)
  local copies, waits for them, and re-layouts  62.5 us (11%)
  other arithmetic  42.9 us (7%)
  starting transfers between devices  19.3 us (3%)
  between operations  14.4 us (3%)
    all_to_all x1, waiting for transfers between devices, body(): lax.all_to_all(row_grad.reshape(groups, capacity, width), 'expert', split...  135 us
    all_to_all x1, waiting for transfers between devices, body(): lax.all_to_all(send_g, 'expert', split_axis=0, concat_axis=0, tiled=True)  124 us
    all_to_all x1, waiting for transfers between devices, body(): lax.all_to_all(send_x, 'expert', split_axis=0, concat_axis=0, tiled=True)  102 us
    scatter x1, other arithmetic, body(): jnp.zeros((groups * capacity, width), jnp.bfloat16).at[target].set(scaled)  22.6 us
    gather x1, local copies, waits for them, and re-layouts, body(): picked = returned.reshape(-1, width)[target]  20.1 us
    scatter x1, local copies, waits for them, and re-layouts, body(): jnp.zeros((groups * capacity, width), jnp.bfloat16).at[target]  18.2 us
    mul x3, local copies, waits for them, and re-layouts, body(): route_weight[:, :, None] * cotangent[:, None, :].astype(jnp.float32)  14.8 us
    dot_general x1, matrix products, body(): lax.dot_general(columns, pre_grad, (((0,), (0,)), ((), ())), preferred_el...  14.2 us
  transfers between devices with their start and end apart: 5, of which 3 were waited for; matrix products, arithmetic and copies ran while one was open for 19% of the time, Pallas kernels for 0%

commit v1 on v0

v1 whole, which is shorter than its diff:
```python
import functools

import jax
import jax.numpy as jnp
from jax import lax
from jax.experimental import pallas as pl
from jax.experimental.pallas import tpu as pltpu
from jax.sharding import PartitionSpec as P

SIDE = 4
OFFSETS = (0, 1, 3, 2)
SLOTS = 72
BOTH = ("dp", "expert")
VMEM_LIMIT = 48 * 1024 * 1024


def ring(first, shift):
    pairs = []
    for dp in range(8):
        along_x = first == (dp % 2 == 0)
        for y in range(SIDE):
            for x in range(SIDE):
                to = y * SIDE + (x + shift) % SIDE if along_x else ((y + shift) % SIDE) * SIDE + x
                pairs.append((dp * 16 + y * SIDE + x, dp * 16 + to))
    return pairs


def send(value, first, shift):
    shift = shift % SIDE
    return value if shift == 0 else lax.ppermute(value, BOTH, ring(first, shift))


def route_kernel(dest_ref, m0, m1, m2, m3, pick_ref, put_ref, weight_ref):
    rows = lax.broadcasted_iota(jnp.int32, (16, 128), 0)
    masks = jnp.zeros((16, 128), jnp.float32)
    weights = []
    for i, meta in enumerate((m0, m1, m2, m3)):
        ids, route = meta[0:8, :], meta[8:16, :]
        for j in range(SIDE):
            hit = ids == dest_ref[j].astype(jnp.float32)
            mask = jnp.sum(jnp.where(hit, 1.0, 0.0), axis=0, keepdims=True)
            weights.append(jnp.sum(jnp.where(hit, route, 0.0), axis=0, keepdims=True))
            masks = jnp.where(rows == i * SIDE + j, mask, masks)
    before = lax.broadcasted_iota(jnp.int32, (128, 128), 0) < lax.broadcasted_iota(
        jnp.int32, (128, 128), 1
    )
    rank = jnp.dot(
        masks.astype(jnp.bfloat16),
        before.astype(jnp.float32).astype(jnp.bfloat16),
        preferred_element_type=jnp.float32,
    )
    rank = jnp.where(masks > 0.5, rank, -1.0)
    slot = lax.broadcasted_iota(jnp.int32, (SLOTS, 128), 0).astype(jnp.float32)
    for i in range(SIDE):
        for j in range(SIDE):
            n = i * SIDE + j
            pick = jnp.where(slot == rank[n : n + 1, :], 1.0, 0.0)
            pick_ref[i, j * SLOTS : (j + 1) * SLOTS, :] = pick.astype(jnp.bfloat16)
            put_ref[i, j, :, :] = pick.T.astype(jnp.bfloat16)
            column = jnp.sum(pick * weights[n], axis=1, keepdims=True)
            weight_ref[i, j * SLOTS : (j + 1) * SLOTS, :] = jnp.broadcast_to(column, (SLOTS, 128))


def route(dest, metas):
    return pl.pallas_call(
        route_kernel,
        out_shape=(
            jax.ShapeDtypeStruct((SIDE, SIDE * SLOTS, 128), jnp.bfloat16),
            jax.ShapeDtypeStruct((SIDE, SIDE, 128, SLOTS), jnp.bfloat16),
            jax.ShapeDtypeStruct((SIDE, SIDE * SLOTS, 128), jnp.float32),
        ),
        in_specs=[pl.BlockSpec(memory_space=pltpu.SMEM)]
        + [pl.BlockSpec(memory_space=pltpu.VMEM)] * 4,
        out_specs=(pl.BlockSpec(memory_space=pltpu.VMEM),) * 3,
        name="route",
    )(dest, *metas)


def select_kernel(scaled, pick_ref, weight_ref, b0, b1, b2, b3, o0, o1, o2, o3):
    outs = (o0, o1, o2, o3)
    for i, block in enumerate((b0, b1, b2, b3)):
        rows = jnp.dot(pick_ref[i], block[...], preferred_element_type=jnp.float32)
        if scaled:
            rows = rows * weight_ref[i][:, 0:1]
        rows = rows.astype(jnp.bfloat16)
        for j in range(SIDE):
            outs[j][i, :, :] = rows[j * SLOTS : (j + 1) * SLOTS, :]


def select(pick, weight, blocks, scaled):
    width = blocks[0].shape[1]
    tile = 512
    return pl.pallas_call(
        functools.partial(select_kernel, scaled),
        out_shape=(jax.ShapeDtypeStruct((SIDE, SLOTS, width), jnp.bfloat16),) * SIDE,
        grid=(width // tile,),
        in_specs=[
            pl.BlockSpec((SIDE, SIDE * SLOTS, 128), lambda c: (0, 0, 0)),
            pl.BlockSpec((SIDE, SIDE * SLOTS, 128), lambda c: (0, 0, 0)),
        ]
        + [pl.BlockSpec((128, tile), lambda c: (0, c))] * SIDE,
        out_specs=(pl.BlockSpec((SIDE, SLOTS, tile), lambda c: (0, 0, c)),) * SIDE,
        compiler_params=pltpu.CompilerParams(vmem_limit_bytes=VMEM_LIMIT),
        cost_estimate=pl.CostEstimate(
            flops=2 * 1152 * 128 * width, bytes_accessed=1664 * width * 2, transcendentals=0
        ),
        name="select_scaled" if scaled else "select",
    )(pick, weight, *blocks)


def combine_kernel(put_ref, r0, r1, r2, r3, o0, o1, o2, o3):
    returned = (r0, r1, r2, r3)
    for i, out in enumerate((o0, o1, o2, o3)):
        total = jnp.dot(put_ref[i, 0], r0[i], preferred_element_type=jnp.float32)
        for j in range(1, SIDE):
            total += jnp.dot(put_ref[i, j], returned[j][i], preferred_element_type=jnp.float32)
        out[...] = total.astype(jnp.bfloat16)


def combine(put, returned):
    width = returned[0].shape[2]
    tile = 512
    return pl.pallas_call(
        combine_kernel,
        out_shape=(jax.ShapeDtypeStruct((128, width), jnp.bfloat16),) * SIDE,
        grid=(width // tile,),
        in_specs=[pl.BlockSpec((SIDE, SIDE, 128, SLOTS), lambda c: (0, 0, 0, 0))]
        + [pl.BlockSpec((SIDE, SLOTS, tile), lambda c: (0, 0, c))] * SIDE,
        out_specs=(pl.BlockSpec((128, tile), lambda c: (0, c)),) * SIDE,
        compiler_params=pltpu.CompilerParams(vmem_limit_bytes=VMEM_LIMIT),
        cost_estimate=pl.CostEstimate(
            flops=2 * 1152 * 128 * width, bytes_accessed=1664 * width * 2, transcendentals=0
        ),
        name="combine",
    )(put, *returned)


ROWS_FIRST = (((0,), (0,)), ((), ()))


def up_kernel(x0, x1, x2, x3, p0, p1, p2, p3, out):
    total = None
    for x, p in ((x0, p0), (x1, p1), (x2, p2), (x3, p3)):
        part = lax.dot_general(x[...], p[...], ROWS_FIRST, preferred_element_type=jnp.float32)
        total = part if total is None else total + part
    out[...] = total.astype(jnp.bfloat16)


def down_kernel(a0, a1, a2, a3, g0, g1, g2, g3, out):
    total = None
    for a, g in ((a0, g0), (a1, g1), (a2, g2), (a3, g3)):
        part = lax.dot_general(a[...], g[...], ROWS_FIRST, preferred_element_type=jnp.float32)
        total = part if total is None else total + part
    out[...] = total.astype(jnp.bfloat16)


def weight_grad(kernel, wide, narrow, wide_first):
    rows, width = wide[0].shape
    hidden = narrow[0].shape[1]
    tile = 512
    wide_specs = [pl.BlockSpec((rows, tile), lambda c: (0, c))] * SIDE
    narrow_specs = [pl.BlockSpec((rows, hidden), lambda c: (0, 0))] * SIDE
    cost = pl.CostEstimate(
        flops=2 * SIDE * rows * width * hidden,
        bytes_accessed=2 * (SIDE * rows * (width + hidden) + width * hidden),
        transcendentals=0,
    )
    params = pltpu.CompilerParams(vmem_limit_bytes=VMEM_LIMIT)
    if wide_first:
        return pl.pallas_call(
            kernel,
            out_shape=jax.ShapeDtypeStruct((width, hidden), jnp.bfloat16),
            grid=(width // tile,),
            in_specs=wide_specs + narrow_specs,
            out_specs=pl.BlockSpec((tile, hidden), lambda c: (c, 0)),
            compiler_params=params,
            cost_estimate=cost,
            name="up_grad",
        )(*wide, *narrow)
    return pl.pallas_call(
        kernel,
        out_shape=jax.ShapeDtypeStruct((hidden, width), jnp.bfloat16),
        grid=(width // tile,),
        in_specs=narrow_specs + wide_specs,
        out_specs=pl.BlockSpec((hidden, tile), lambda c: (0, c)),
        compiler_params=params,
        cost_estimate=cost,
        name="down_grad",
    )(*narrow, *wide)


def body(tokens, cotangent, expert_ids, route_weight, up_weight, down_weight):
    width = tokens.shape[1]
    up_matrix = up_weight[0]
    down_matrix = down_weight[0]
    odd = lax.axis_index("dp") % 2 == 1
    place = lax.axis_index("expert")
    y, x = place // SIDE, place % SIDE
    shifts = jnp.array(OFFSETS, jnp.int32)
    dest = jnp.where(odd, y * SIDE + (x + shifts) % SIDE, ((y + shifts) % SIDE) * SIDE + x)
    meta = jnp.concatenate([expert_ids.astype(jnp.float32).T, route_weight.T], axis=0)

    metas = [send(meta, True, o) for o in OFFSETS]
    token_blocks = [send(tokens, True, o) for o in OFFSETS]
    cot_blocks = [send(cotangent, True, o) for o in OFFSETS]
    pick, put, weight = route(dest, metas)

    rows_x = select(pick, weight, token_blocks, False)
    rows_x = [send(r, False, o).reshape(SIDE * SLOTS, width) for r, o in zip(rows_x, OFFSETS)]
    rows_g = select(pick, weight, cot_blocks, True)
    rows_g = [send(r, False, o).reshape(SIDE * SLOTS, width) for r, o in zip(rows_g, OFFSETS)]

    actives, grads, returned = [], [], []
    for rx, rg, o in zip(rows_x, rows_g, OFFSETS):
        pre = jnp.dot(rx, up_matrix, preferred_element_type=jnp.float32)
        sigma = jax.nn.sigmoid(pre)
        actives.append((pre * sigma).astype(jnp.bfloat16))
        back = lax.dot_general(
            rg, down_matrix, (((1,), (1,)), ((), ())), preferred_element_type=jnp.float32
        )
        grad = (back * sigma * (1.0 + pre * (1.0 - sigma))).astype(jnp.bfloat16)
        grads.append(grad)
        row_grad = lax.dot_general(
            grad, up_matrix, (((1,), (1,)), ((), ())), preferred_element_type=jnp.float32
        ).astype(jnp.bfloat16)
        returned.append(send(row_grad.reshape(SIDE, SLOTS, width), False, -o))

    up_part = weight_grad(up_kernel, rows_x, grads, True)
    up_grad = lax.psum_scatter(up_part, "dp", scatter_dimension=0, tiled=True)
    down_part = weight_grad(down_kernel, rows_g, actives, False)
    down_grad = lax.psum_scatter(down_part, "dp", scatter_dimension=0, tiled=True)

    parts = combine(put, returned)
    parts = [send(p, True, -o) for p, o in zip(parts, OFFSETS)]
    token_grad = sum(p.astype(jnp.float32) for p in parts).astype(jnp.bfloat16)
    return (
        token_grad,
        up_grad.astype(jnp.float32)[None],
        down_grad.astype(jnp.float32)[None],
    )


def solution(mesh):
    rows = P(("dp", "expert"), None)
    weights = P("expert", None, None)
    return jax.shard_map(
        body,
        mesh=mesh,
        in_specs=(rows, rows, rows, rows, weights, weights),
        out_specs=(rows, P("expert", "dp", None), P("expert", "dp", None)),
        check_vma=False,
    )
```

time: 575 us -> 360 us (0.63); the launches traced: 566 us -> 359 us
  waiting for transfers between devices: 360 us -> 180 us
  Pallas kernels: 0 us -> 58.4 us
  local copies, waits for them, and re-layouts: 62.5 us -> 8 us
  other arithmetic: 42.9 us -> 8.98 us
  starting transfers between devices: 19.3 us -> 38.2 us
  matrix products: 66.7 us -> 51.6 us
    all_to_all x3 -> x0, waiting for transfers between devices: 360 us -> none  [the longest x1 135 us: body(): lax.all_to_all(row_grad.reshape(groups, capacity, width), 'expert', split...]
    ppermute x0 -> x21, waiting for transfers between devices: none -> 180 us  [send(): lax.ppermute(value, BOTH, ring(first, shift))]
    pallas_call x0 -> x6, Pallas kernels: none -> 58.4 us  [the longest x1 17.1 us: weight_grad(): pl.pallas_call(kernel, out_shape=jax.ShapeDtypeStruct((width, hidden), jn...]
    ppermute x0 -> x21, starting transfers between devices: none -> 37.9 us  [send(): lax.ppermute(value, BOTH, ring(first, shift))]
    gather x2 -> x0, local copies, waits for them, and re-layouts: 27.8 us -> none  [the longest x1 20.1 us: body(): picked = returned.reshape(-1, width)[target]]
    scatter x1 -> x0, other arithmetic: 22.6 us -> none  [body(): jnp.zeros((groups * capacity, width), jnp.bfloat16).at[target].set(scaled)]
    all_to_all x3 -> x0, starting transfers between devices: 18.8 us -> none  [the longest x1 7.48 us: body(): lax.all_to_all(send_x, 'expert', split_axis=0, concat_axis=0, tiled=True)]
    scatter x1 -> x0, local copies, waits for them, and re-layouts: 18.2 us -> none  [body(): jnp.zeros((groups * capacity, width), jnp.bfloat16).at[target]]
  transfers between devices with their start and end apart: 5 -> 23, of which waited for: 3 -> 11; matrix products, arithmetic and copies ran while one was open for 19% -> 16% of each run, Pallas kernels for 0% -> 10%
where the time goes in v1:
time: 360 us; the launch traced here: 359 us
  waiting for transfers between devices  180 us (50%)
  Pallas kernels  58.4 us (16%)
  matrix products  51.6 us (14%)
  starting transfers between devices  38.2 us (11%)
  between operations  14.3 us (4%)
  other arithmetic  8.98 us (2%)
  local copies, waits for them, and re-layouts  8 us (2%)
    ppermute x21, waiting for transfers between devices, send(): lax.ppermute(value, BOTH, ring(first, shift))  180 us
    ppermute x21, starting transfers between devices, send(): lax.ppermute(value, BOTH, ring(first, shift))  37.9 us
    dot_general x4, matrix products, body(): lax.dot_general(rg, down_matrix, (((1,), (1,)), ((), ())), preferred_elem...  19.6 us
    pallas_call x1, Pallas kernels, weight_grad(): pl.pallas_call(kernel, out_shape=jax.ShapeDtypeStruct((width, hidden), jn...  17.1 us
    pallas_call x1, Pallas kernels, weight_grad(): pl.pallas_call(kernel, out_shape=jax.ShapeDtypeStruct((hidden, width), jn...  16.9 us
    dot_general x4, matrix products, body(): pre = jnp.dot(rx, up_matrix, preferred_element_type=jnp.float32)  16.8 us
    dot_general x4, matrix products, body(): lax.dot_general(grad, up_matrix, (((1,), (1,)), ((), ())), preferred_elem...  15.3 us
    pallas_call x2, Pallas kernels, select(): pl.pallas_call(functools.partial(select_kernel, scaled), out_shape=(jax.S...  13.3 us
  transfers between devices with their start and end apart: 23, of which 11 were waited for; matrix products, arithmetic and copies ran while one was open for 16% of the time, Pallas kernels for 10%

profile of v1, /device:TPU:0, one launch (start us, length us, event | category | flops | bytes accessed | tf_op | source)
XLA Modules:
  0.0 359.1 jit_solution(15095174025039795775)
XLA Ops:
  17.0 15.7 %collective-permute-done.m1 = f32[16,128]{1,0:T(8,128)S(1)} collective-permute-done((f32[16,128]{1,0:T(8,128)S(1)}, f32[16,128]{1,0:T(8,128)S(1)}, u32[]{:S(2)}, u32[]{:S(2)}) %collective-permute-start) | collective-permute-done | bytes 8224 | tf_op jit(solution)/shard_map/ppermute | solution.py:30
  32.8 4.0 %collective-permute-start.2 = (f32[16,128]{1,0:T(8,128)S(1)}, f32[16,128]{1,0:T(8,128)S(1)}, u32[]{:S(2)}, u32[]{:S(2)}) collective-permute-start(f32[16,128]{1,0:T(8,128)S(1)} %pad_maximum_fusion.m0), channel_id=1, source_target_pairs={{0,2},{1,3},{2,0},{3,1},{4,6},{5,7},{6,4},{7,5},{8,10},{9,11},{10,... | collective-permute-start | bytes 24584 | tf_op jit(solution)/shard_map/ppermute | solution.py:30
  44.5 6.6 %select.13 = (bf16[4,72,4096]{2,1,0:T(8,128)(2,1)}, bf16[4,72,4096]{2,1,0:T(8,128)(2,1)}, bf16[4,72,4096]{2,1,0:T(8,128)(2,1)}, bf16[4,72,4096]{2,1,0:T(8,128)(2,1)}) custom-call(bf16[4,288,128]{2,1,0:T(8,128)(2,1)S(1)} %copy-done.1, f32[4,288,128]{2,1,0:T(8,128)S(1)} %copy-done, bf16[128,4096]{1,0:T(8,128)(2,1)S(1)} %copy-done.2, ...), custom_call_target="tpu_custom_call" | custom-call | flops 1207959552 | bytes 13631488 | tf_op jit(solution)/shard_map/select/pallas_call | solution.py:93
  59.8 20.2 %collective-permute-done.3.b1 = bf16[128,4096]{1,0:T(8,128)(2,1)S(1)} collective-permute-done((bf16[128,4096]{1,0:T(8,128)(2,1)S(1)}, bf16[128,4096]{1,0:T(8,128)(2,1)S(1)}, u32[]{:S(2)}, u32[]{:S(2)}) %collective-permute-start.3) | collective-permute-done | bytes 1048608 | tf_op jit(solution)/shard_map/ppermute | solution.py:30
  82.9 20.9 %collective-permute-done.5.b3 = bf16[128,4096]{1,0:T(8,128)(2,1)S(1)} collective-permute-done((bf16[128,4096]{1,0:T(8,128)(2,1)S(1)}, bf16[128,4096]{1,0:T(8,128)(2,1)S(1)}, u32[]{:S(2)}, u32[]{:S(2)}) %collective-permute-start.5) | collective-permute-done | bytes 1048608 | tf_op jit(solution)/shard_map/ppermute | solution.py:30
  103.9 6.7 %select_scaled.1 = (bf16[4,72,4096]{2,1,0:T(8,128)(2,1)}, bf16[4,72,4096]{2,1,0:T(8,128)(2,1)}, bf16[4,72,4096]{2,1,0:T(8,128)(2,1)}, bf16[4,72,4096]{2,1,0:T(8,128)(2,1)}) custom-call(bf16[4,288,128]{2,1,0:T(8,128)(2,1)S(1)} %copy-done.1, f32[4,288,128]{2,1,0:T(8,128)S(1)} %copy-done, bf16[128,4096]{1,0:T(8,128)(2,1)S(1)} %copy-done.3, ...), custom_call_target="tpu_custom_call" | custom-call | flops 1207959552 | bytes 13631488 | tf_op jit(solution)/shard_map/select_scaled/pallas_call | solution.py:93
  117.8 4.6 %multiply_convert_fusion.2 = (bf16[288,768]{1,0:T(8,128)(2,1)S(1)}, f32[288,768]{1,0:T(8,128)}) fusion(bf16[288,4096]{1,0:T(8,128)(2,1)} %bitcast.8.x1, bf16[1,4096,768]{2,1,0:T(8,128)(2,1)S(1)} %copy-done.18), kind=kOutput, calls=%fused_computation.43 | convolution fusion | flops 1813045248 | bytes 9977856 | tf_op jit(solution)/shard_map/dot_general | solution.py:215
  122.4 5.1 %collective-permute-done.13 = bf16[4,72,4096]{2,1,0:T(8,128)(2,1)} collective-permute-done((bf16[4,72,4096]{2,1,0:T(8,128)(2,1)}, bf16[4,72,4096]{2,1,0:T(8,128)(2,1)}, u32[]{:S(2)}, u32[]{:S(2)}) %collective-permute-start.13) | collective-permute-done | bytes 2359328 | tf_op jit(solution)/shard_map/ppermute | solution.py:30
  127.5 4.6 %multiply_convert_fusion.1 = (bf16[288,768]{1,0:T(8,128)(2,1)S(1)}, f32[288,768]{1,0:T(8,128)}) fusion(bf16[288,4096]{1,0:T(8,128)(2,1)} %bitcast.11.x2, bf16[1,4096,768]{2,1,0:T(8,128)(2,1)S(1)} %copy-done.18), kind=kOutput, calls=%fused_computation.42 | convolution fusion | flops 1813045248 | bytes 9977856 | tf_op jit(solution)/shard_map/dot_general | solution.py:215
  132.1 4.7 %multiply_convert_fusion = (bf16[288,768]{1,0:T(8,128)(2,1)S(1)}, f32[288,768]{1,0:T(8,128)}) fusion(bf16[288,4096]{1,0:T(8,128)(2,1)} %bitcast.14.x3, bf16[1,4096,768]{2,1,0:T(8,128)(2,1)S(1)} %copy-done.18), kind=kOutput, calls=%fused_computation.41 | convolution fusion | flops 1813045248 | bytes 9977856 | tf_op jit(solution)/shard_map/dot_general | solution.py:215
  136.8 41.3 %collective-permute-done.12 = bf16[4,72,4096]{2,1,0:T(8,128)(2,1)} collective-permute-done((bf16[4,72,4096]{2,1,0:T(8,128)(2,1)}, bf16[4,72,4096]{2,1,0:T(8,128)(2,1)}, u32[]{:S(2)}, u32[]{:S(2)}) %collective-permute-start.12) | collective-permute-done | bytes 2359328 | tf_op jit(solution)/shard_map/ppermute | solution.py:30
  179.3 16.9 %down_grad.1 = bf16[768,4096]{1,0:T(8,128)(2,1)} custom-call(bf16[288,768]{1,0:T(8,128)(2,1)S(1)} %get-tuple-element.33.a0, bf16[288,768]{1,0:T(8,128)(2,1)S(1)} %get-tuple-element.35.a1, bf16[288,768]{1,0:T(8,128)(2,1)S(1)} %get-tuple-element.37.a2, bf16[288,768]{1,0:T(8,128)(2,1)S(1)} %get-tuple-element.39.a3, bf16[288,4096]{1,0:T(8,128)(2,1)S(1)} %bitcast.102, ...), custom_call_target="tpu_custom_call" | custom-call | flops 7247757312 | bytes 17498112 | tf_op jit(solution)/shard_map/down_grad/pallas_call | solution.py:180
  196.6 5.9 %fusion.69.p0 = bf16[288,768]{1,0:T(8,128)(2,1)S(1)} fusion(bf16[288,4096]{1,0:T(8,128)(2,1)} %bitcast.101, bf16[1,768,4096]{2,1,0:T(8,128)(2,1)} %param.12, f32[288,768]{1,0:T(8,128)} %get-tuple-element.34), kind=kOutput, calls=%fused_computation.40 | convolution fusion | flops 1813929984 | bytes 9977856 | tf_op jit(solution)/shard_map/dot_general | solution.py:218
  202.5 5.8 %fusion.60.p3 = bf16[288,768]{1,0:T(8,128)(2,1)S(1)} fusion(bf16[288,4096]{1,0:T(8,128)(2,1)} %bitcast.13.g3, bf16[1,768,4096]{2,1,0:T(8,128)(2,1)} %param.12, f32[288,768]{1,0:T(8,128)S(1)} %copy-done.21), kind=kOutput, calls=%fused_computation.37 | convolution fusion | flops 1813929984 | bytes 9977856 | tf_op jit(solution)/shard_map/dot_general | solution.py:218
  208.3 3.9 %fusion.63.p2 = bf16[288,768]{1,0:T(8,128)(2,1)S(1)} fusion(bf16[288,4096]{1,0:T(8,128)(2,1)} %bitcast.10.g2, bf16[1,768,4096]{2,1,0:T(8,128)(2,1)S(1)} %bitcast.106, f32[288,768]{1,0:T(8,128)S(1)} %copy-done.20), kind=kOutput, calls=%fused_computation.38 | convolution fusion | flops 1813929984 | bytes 9977856 | tf_op jit(solution)/shard_map/dot_general | solution.py:218
  212.3 4.0 %fusion.66.p1 = bf16[288,768]{1,0:T(8,128)(2,1)S(1)} fusion(bf16[288,4096]{1,0:T(8,128)(2,1)} %bitcast.7.g1, bf16[1,768,4096]{2,1,0:T(8,128)(2,1)S(1)} %bitcast.106, f32[288,768]{1,0:T(8,128)S(1)} %copy-done.19), kind=kOutput, calls=%fused_computation.39 | convolution fusion | flops 1813929984 | bytes 9977856 | tf_op jit(solution)/shard_map/dot_general | solution.py:218
  216.3 17.1 %up_grad.1 = bf16[4096,768]{1,0:T(8,128)(2,1)} custom-call(bf16[288,4096]{1,0:T(8,128)(2,1)S(1)} %bitcast.100, bf16[288,4096]{1,0:T(8,128)(2,1)} %bitcast.8.x1, bf16[288,4096]{1,0:T(8,128)(2,1)} %bitcast.11.x2, bf16[288,4096]{1,0:T(8,128)(2,1)} %bitcast.14.x3, bf16[288,768]{1,0:T(8,128)(2,1)S(1)} %fusion.69.p0, bf16[288,768]{1,0:T(8,128)(2,1)S(1)} %fusion.66.p1, ...), custom_call_target="tpu_custom_call" | custom-call | flops 7247757312 | bytes 17498112 | tf_op jit(solution)/shard_map/up_grad/pallas_call | solution.py:170
  235.1 5.0 %fusion.27 = bf16[288,4096]{1,0:T(8,128)(2,1)S(1)} fusion(bf16[288,768]{1,0:T(8,128)(2,1)S(1)} %copy-done.10, bf16[1,4096,768]{2,1,0:T(8,128)(2,1)} %param.11), kind=kOutput, calls=%fused_computation.25 | convolution fusion | flops 1813118976 | bytes 9093120 | tf_op jit(solution)/shard_map/dot_general | solution.py:223
  243.0 4.8 %fusion.30 = bf16[288,4096]{1,0:T(8,128)(2,1)S(1)} fusion(bf16[288,768]{1,0:T(8,128)(2,1)S(1)} %copy-done.8, bf16[1,4096,768]{2,1,0:T(8,128)(2,1)} %param.11), kind=kOutput, calls=%fused_computation.26 | convolution fusion | flops 1813118976 | bytes 9093120 | tf_op jit(solution)/shard_map/dot_general | solution.py:223
  255.2 39.5 %collective-permute-done.11.r1 = bf16[4,72,4096]{2,1,0:T(8,128)(2,1)S(1)} collective-permute-done((bf16[4,72,4096]{2,1,0:T(8,128)(2,1)S(1)}, bf16[4,72,4096]{2,1,0:T(8,128)(2,1)S(1)}, u32[]{:S(2)}, u32[]{:S(2)}) %collective-permute-start.11) | collective-permute-done | bytes 2359328 | tf_op jit(solution)/shard_map/ppermute | solution.py:30
  294.7 10.6 %collective-permute-done.14.r2 = bf16[4,72,4096]{2,1,0:T(8,128)(2,1)S(1)} collective-permute-done((bf16[4,72,4096]{2,1,0:T(8,128)(2,1)S(1)}, bf16[4,72,4096]{2,1,0:T(8,128)(2,1)S(1)}, u32[]{:S(2)}, u32[]{:S(2)}) %collective-permute-start.14) | collective-permute-done | bytes 2359328 | tf_op jit(solution)/shard_map/ppermute | solution.py:30
  307.5 8.9 %combine.1 = (bf16[128,4096]{1,0:T(8,128)(2,1)S(1)}, bf16[128,4096]{1,0:T(8,128)(2,1)S(1)}, bf16[128,4096]{1,0:T(8,128)(2,1)S(1)}, bf16[128,4096]{1,0:T(8,128)(2,1)S(1)}) custom-call(bf16[4,4,128,72]{3,2,1,0:T(8,128)(2,1)S(1)} %copy-done.4, bf16[4,72,4096]{2,1,0:T(8,128)(2,1)} %bitcast.103, bf16[4,72,4096]{2,1,0:T(8,128)(2,1)} %copy-done.11, ...), custom_call_target="tpu_custom_call" | custom-call | flops 1207959552 | bytes 13631488 | tf_op jit(solution)/shard_map/combine/pallas_call | solution.py:123
  321.3 20.9 %collective-permute-done.18 = bf16[128,4096]{1,0:T(8,128)(2,1)S(1)} collective-permute-done((bf16[128,4096]{1,0:T(8,128)(2,1)S(1)}, bf16[128,4096]{1,0:T(8,128)(2,1)S(1)}, u32[]{:S(2)}, u32[]{:S(2)}) %collective-permute-start.18) | collective-permute-done | bytes 1048608 | tf_op jit(solution)/shard_map/ppermute | solution.py:30
  342.1 3.7 %collective-permute-done.19 = bf16[128,4096]{1,0:T(8,128)(2,1)S(1)} collective-permute-done((bf16[128,4096]{1,0:T(8,128)(2,1)S(1)}, bf16[128,4096]{1,0:T(8,128)(2,1)S(1)}, u32[]{:S(2)}, u32[]{:S(2)}) %collective-permute-start.19) | collective-permute-done | bytes 1048608 | tf_op jit(solution)/shard_map/ppermute | solution.py:30
  (102 shorter events, 63.5 us)
Async XLA Ops:
  7.2 340.3 %reduce-scatter.5.cloned.1.call-start = ((), (), s32[]{:S(2)}) async-start(), calls=%async_computation.3 | async-start | bytes 7077888 | tf_op jit(solution)/shard_map/reduce_scatter | solution.py:231
  7.2 34.0 %collective-permute-start.6 = (bf16[128,4096]{1,0:T(8,128)(2,1)}, bf16[128,4096]{1,0:T(8,128)(2,1)S(1)}, u32[]{:S(2)}, u32[]{:S(2)}) collective-permute-start(bf16[128,4096]{1,0:T(8,128)(2,1)} %b0.3), channel_id=1, source_target_pairs={{0,1},{1,2},{2,3},{3,0},{4,5},{5,6},{6,7},{7,4},{8,9},{9,10},{10,1... | collective-permute-start | bytes 3145736 | tf_op jit(solution)/shard_map/ppermute | solution.py:30
  8.9 32.4 %collective-permute-start.7 = (bf16[128,4096]{1,0:T(8,128)(2,1)}, bf16[128,4096]{1,0:T(8,128)(2,1)S(1)}, u32[]{:S(2)}, u32[]{:S(2)}) collective-permute-start(bf16[128,4096]{1,0:T(8,128)(2,1)} %b0.3), channel_id=1, source_target_pairs={{0,3},{1,0},{2,1},{3,2},{4,7},{5,4},{6,5},{7,6},{8,11},{9,8},{10,9... | collective-permute-start | bytes 3145736 | tf_op jit(solution)/shard_map/ppermute | solution.py:30
  10.5 30.7 %collective-permute-start.8 = (bf16[128,4096]{1,0:T(8,128)(2,1)}, bf16[128,4096]{1,0:T(8,128)(2,1)S(1)}, u32[]{:S(2)}, u32[]{:S(2)}) collective-permute-start(bf16[128,4096]{1,0:T(8,128)(2,1)} %b0.3), channel_id=1, source_target_pairs={{0,2},{1,3},{2,0},{3,1},{4,6},{5,7},{6,4},{7,5},{8,10},{9,11},{10,... | collective-permute-start | bytes 3145736 | tf_op jit(solution)/shard_map/ppermute | solution.py:30
  13.8 19.0 %collective-permute-start = (f32[16,128]{1,0:T(8,128)S(1)}, f32[16,128]{1,0:T(8,128)S(1)}, u32[]{:S(2)}, u32[]{:S(2)}) collective-permute-start(f32[16,128]{1,0:T(8,128)S(1)} %pad_maximum_fusion.m0), channel_id=1, source_target_pairs={{0,1},{1,2},{2,3},{3,0},{4,5},{5,6},{6,7},{7,4},{8,9},{9,10},{10,1... | collective-permute-start | bytes 24584 | tf_op jit(solution)/shard_map/ppermute | solution.py:30
  14.4 23.5 %collective-permute-start.1 = (f32[16,128]{1,0:T(8,128)S(1)}, f32[16,128]{1,0:T(8,128)S(1)}, u32[]{:S(2)}, u32[]{:S(2)}) collective-permute-start(f32[16,128]{1,0:T(8,128)S(1)} %pad_maximum_fusion.m0), channel_id=1, source_target_pairs={{0,3},{1,0},{2,1},{3,2},{4,7},{5,4},{6,5},{7,6},{8,11},{9,8},{10,9... | collective-permute-start | bytes 24584 | tf_op jit(solution)/shard_map/ppermute | solution.py:30
  32.8 5.6 %collective-permute-start.2 = (f32[16,128]{1,0:T(8,128)S(1)}, f32[16,128]{1,0:T(8,128)S(1)}, u32[]{:S(2)}, u32[]{:S(2)}) collective-permute-start(f32[16,128]{1,0:T(8,128)S(1)} %pad_maximum_fusion.m0), channel_id=1, source_target_pairs={{0,2},{1,3},{2,0},{3,1},{4,6},{5,7},{6,4},{7,5},{8,10},{9,11},{10,... | collective-permute-start | bytes 24584 | tf_op jit(solution)/shard_map/ppermute | solution.py:30
  44.5 70.4 %copy-start.18 = (bf16[1,4096,768]{2,1,0:T(8,128)(2,1)S(1)}, bf16[1,4096,768]{2,1,0:T(8,128)(2,1)}, u32[]{:S(2)}) copy-start(bf16[1,4096,768]{2,1,0:T(8,128)(2,1)} %param.11) | copy-start | bytes 18874372
  51.2 63.1 %collective-permute-start.10 = (bf16[4,72,4096]{2,1,0:T(8,128)(2,1)}, bf16[4,72,4096]{2,1,0:T(8,128)(2,1)}, u32[]{:S(2)}, u32[]{:S(2)}) collective-permute-start(bf16[4,72,4096]{2,1,0:T(8,128)(2,1)} %get-tuple-element.24), channel_id=1, source_target_pairs={{0,4},{1,5},{2,6},{3,7},{4,8},{5,9},{6,10},{7,11},{8,12},{9,13},{1... | collective-permute-start | bytes 7077896 | tf_op jit(solution)/shard_map/ppermute | solution.py:30
  52.7 27.3 %collective-permute-start.3 = (bf16[128,4096]{1,0:T(8,128)(2,1)S(1)}, bf16[128,4096]{1,0:T(8,128)(2,1)S(1)}, u32[]{:S(2)}, u32[]{:S(2)}) collective-permute-start(bf16[128,4096]{1,0:T(8,128)(2,1)S(1)} %copy-done.3), channel_id=1, source_target_pairs={{0,1},{1,2},{2,3},{3,0},{4,5},{5,6},{6,7},{7,4},{8,9},{9,10},{10,1... | collective-permute-start | bytes 3145736 | tf_op jit(solution)/shard_map/ppermute | solution.py:30
  54.7 28.3 %collective-permute-start.4 = (bf16[128,4096]{1,0:T(8,128)(2,1)S(1)}, bf16[128,4096]{1,0:T(8,128)(2,1)S(1)}, u32[]{:S(2)}, u32[]{:S(2)}) collective-permute-start(bf16[128,4096]{1,0:T(8,128)(2,1)S(1)} %copy-done.3), channel_id=1, source_target_pairs={{0,3},{1,0},{2,1},{3,2},{4,7},{5,4},{6,5},{7,6},{8,11},{9,8},{10,9... | collective-permute-start | bytes 3145736 | tf_op jit(solution)/shard_map/ppermute | solution.py:30
  56.0 47.9 %collective-permute-start.5 = (bf16[128,4096]{1,0:T(8,128)(2,1)S(1)}, bf16[128,4096]{1,0:T(8,128)(2,1)S(1)}, u32[]{:S(2)}, u32[]{:S(2)}) collective-permute-start(bf16[128,4096]{1,0:T(8,128)(2,1)S(1)} %copy-done.3), channel_id=1, source_target_pairs={{0,2},{1,3},{2,0},{3,1},{4,6},{5,7},{6,4},{7,5},{8,10},{9,11},{10,... | collective-permute-start | bytes 3145736 | tf_op jit(solution)/shard_map/ppermute | solution.py:30
  58.2 69.3 %collective-permute-start.13 = (bf16[4,72,4096]{2,1,0:T(8,128)(2,1)}, bf16[4,72,4096]{2,1,0:T(8,128)(2,1)}, u32[]{:S(2)}, u32[]{:S(2)}) collective-permute-start(bf16[4,72,4096]{2,1,0:T(8,128)(2,1)} %get-tuple-element.26), channel_id=1, source_target_pairs={{0,12},{1,13},{2,14},{3,15},{4,0},{5,1},{6,2},{7,3},{8,4},{9,5},{1... | collective-permute-start | bytes 7077896 | tf_op jit(solution)/shard_map/ppermute | solution.py:30
  80.0 52.0 %collective-permute-start.16 = (bf16[4,72,4096]{2,1,0:T(8,128)(2,1)}, bf16[4,72,4096]{2,1,0:T(8,128)(2,1)}, u32[]{:S(2)}, u32[]{:S(2)}) collective-permute-start(bf16[4,72,4096]{2,1,0:T(8,128)(2,1)} %get-tuple-element.28), channel_id=1, source_target_pairs={{0,8},{1,9},{2,10},{3,11},{4,12},{5,13},{6,14},{7,15},{8,0},{9,1},... | collective-permute-start | bytes 7077896 | tf_op jit(solution)/shard_map/ppermute | solution.py:30
  110.6 67.5 %collective-permute-start.12 = (bf16[4,72,4096]{2,1,0:T(8,128)(2,1)}, bf16[4,72,4096]{2,1,0:T(8,128)(2,1)}, u32[]{:S(2)}, u32[]{:S(2)}) collective-permute-start(bf16[4,72,4096]{2,1,0:T(8,128)(2,1)} %get-tuple-element.25), channel_id=1, source_target_pairs={{0,12},{1,13},{2,14},{3,15},{4,0},{5,1},{6,2},{7,3},{8,4},{9,5},{1... | collective-permute-start | bytes 7077896 | tf_op jit(solution)/shard_map/ppermute | solution.py:30
  112.2 65.8 %collective-permute-start.15 = (bf16[4,72,4096]{2,1,0:T(8,128)(2,1)}, bf16[4,72,4096]{2,1,0:T(8,128)(2,1)}, u32[]{:S(2)}, u32[]{:S(2)}) collective-permute-start(bf16[4,72,4096]{2,1,0:T(8,128)(2,1)} %get-tuple-element.27), channel_id=1, source_target_pairs={{0,8},{1,9},{2,10},{3,11},{4,12},{5,13},{6,14},{7,15},{8,0},{9,1},... | collective-permute-start | bytes 7077896 | tf_op jit(solution)/shard_map/ppermute | solution.py:30
  114.2 65.1 %collective-permute-start.9 = (bf16[4,72,4096]{2,1,0:T(8,128)(2,1)}, bf16[4,72,4096]{2,1,0:T(8,128)(2,1)}, u32[]{:S(2)}, u32[]{:S(2)}) collective-permute-start(bf16[4,72,4096]{2,1,0:T(8,128)(2,1)} %get-tuple-element.23), channel_id=1, source_target_pairs={{0,4},{1,5},{2,6},{3,7},{4,8},{5,9},{6,10},{7,11},{8,12},{9,13},{1... | collective-permute-start | bytes 7077896 | tf_op jit(solution)/shard_map/ppermute | solution.py:30
  196.3 153.6 %reduce-scatter.3.cloned.1.call-start = ((), (), s32[]{:S(2)}) async-start(), calls=%async_computation.2 | async-start | bytes 7077888 | tf_op jit(solution)/shard_map/reduce_scatter | solution.py:229
  240.1 54.5 %collective-permute-start.11 = (bf16[4,72,4096]{2,1,0:T(8,128)(2,1)S(1)}, bf16[4,72,4096]{2,1,0:T(8,128)(2,1)S(1)}, u32[]{:S(2)}, u32[]{:S(2)}) collective-permute-start(bf16[4,72,4096]{2,1,0:T(8,128)(2,1)S(1)} %bitcast.109), channel_id=1, source_target_pairs={{0,12},{1,13},{2,14},{3,15},{4,0},{5,1},{6,2},{7,3},{8,4},{9,5},{1... | collective-permute-start | bytes 7077896 | tf_op jit(solution)/shard_map/ppermute | solution.py:30
  249.9 55.4 %collective-permute-start.14 = (bf16[4,72,4096]{2,1,0:T(8,128)(2,1)S(1)}, bf16[4,72,4096]{2,1,0:T(8,128)(2,1)S(1)}, u32[]{:S(2)}, u32[]{:S(2)}) collective-permute-start(bf16[4,72,4096]{2,1,0:T(8,128)(2,1)S(1)} %bitcast.111), channel_id=1, source_target_pairs={{0,4},{1,5},{2,6},{3,7},{4,8},{5,9},{6,10},{7,11},{8,12},{9,13},{1... | collective-permute-start | bytes 7077896 | tf_op jit(solution)/shard_map/ppermute | solution.py:30
  250.1 55.2 %collective-permute-start.17 = (bf16[4,72,4096]{2,1,0:T(8,128)(2,1)S(1)}, bf16[4,72,4096]{2,1,0:T(8,128)(2,1)S(1)}, u32[]{:S(2)}, u32[]{:S(2)}) collective-permute-start(bf16[4,72,4096]{2,1,0:T(8,128)(2,1)S(1)} %bitcast.110), channel_id=1, source_target_pairs={{0,8},{1,9},{2,10},{3,11},{4,12},{5,13},{6,14},{7,15},{8,0},{9,1},... | collective-permute-start | bytes 7077896 | tf_op jit(solution)/shard_map/ppermute | solution.py:30
  316.4 25.7 %collective-permute-start.18 = (bf16[128,4096]{1,0:T(8,128)(2,1)S(1)}, bf16[128,4096]{1,0:T(8,128)(2,1)S(1)}, u32[]{:S(2)}, u32[]{:S(2)}) collective-permute-start(bf16[128,4096]{1,0:T(8,128)(2,1)S(1)} %get-tuple-element.30), channel_id=1, source_target_pairs={{0,3},{1,0},{2,1},{3,2},{4,7},{5,4},{6,5},{7,6},{8,11},{9,8},{10,9... | collective-permute-start | bytes 3145736 | tf_op jit(solution)/shard_map/ppermute | solution.py:30
  318.6 27.2 %collective-permute-start.19 = (bf16[128,4096]{1,0:T(8,128)(2,1)S(1)}, bf16[128,4096]{1,0:T(8,128)(2,1)S(1)}, u32[]{:S(2)}, u32[]{:S(2)}) collective-permute-start(bf16[128,4096]{1,0:T(8,128)(2,1)S(1)} %get-tuple-element.31), channel_id=1, source_target_pairs={{0,1},{1,2},{2,3},{3,0},{4,5},{5,6},{6,7},{7,4},{8,9},{9,10},{10,1... | collective-permute-start | bytes 3145736 | tf_op jit(solution)/shard_map/ppermute | solution.py:30
  318.6 27.2 %collective-permute-start.20 = (bf16[128,4096]{1,0:T(8,128)(2,1)S(1)}, bf16[128,4096]{1,0:T(8,128)(2,1)S(1)}, u32[]{:S(2)}, u32[]{:S(2)}) collective-permute-start(bf16[128,4096]{1,0:T(8,128)(2,1)S(1)} %get-tuple-element.32), channel_id=1, source_target_pairs={{0,2},{1,3},{2,0},{3,1},{4,6},{5,7},{6,4},{7,5},{8,10},{9,11},{10,... | collective-permute-start | bytes 3145736 | tf_op jit(solution)/shard_map/ppermute | solution.py:30
  (25 other events, 258.9 us)
Sparse Core Ops, SparseCore 0:
  196.4 45.6 reduce-scatter.4
  244.5 42.3 reduce-scatter.2

commit v2 on v1

v2 whole, which is shorter than its diff:
```python
import functools

import jax
import jax.numpy as jnp
from jax import lax
from jax.experimental import pallas as pl
from jax.experimental.pallas import tpu as pltpu
from jax.sharding import PartitionSpec as P

SIDE = 4
OFFSETS = (0, 1, 3, 2)
SLOTS = 72
BOTH = ("dp", "expert")
VMEM_LIMIT = 40 * 1024 * 1024
FREE = pl.CostEstimate(flops=1, bytes_accessed=1, transcendentals=0)
PARAMS = pltpu.CompilerParams(vmem_limit_bytes=VMEM_LIMIT)


def ring(first, shift):
    pairs = []
    for dp in range(8):
        along_x = first == (dp % 2 == 0)
        for y in range(SIDE):
            for x in range(SIDE):
                to = y * SIDE + (x + shift) % SIDE if along_x else ((y + shift) % SIDE) * SIDE + x
                pairs.append((dp * 16 + y * SIDE + x, dp * 16 + to))
    return pairs


def send(value, first, shift):
    shift = shift % SIDE
    return value if shift == 0 else lax.ppermute(value, BOTH, ring(first, shift))


def route_kernel(dest_ref, m0, m1, m2, m3, pick_ref, put_ref, weight_ref):
    rows = lax.broadcasted_iota(jnp.int32, (16, 128), 0)
    masks = jnp.zeros((16, 128), jnp.float32)
    weights = []
    for i, meta in enumerate((m0, m1, m2, m3)):
        ids, route = meta[0:8, :], meta[8:16, :]
        for j in range(SIDE):
            hit = ids == dest_ref[j].astype(jnp.float32)
            mask = jnp.sum(jnp.where(hit, 1.0, 0.0), axis=0, keepdims=True)
            weights.append(jnp.sum(jnp.where(hit, route, 0.0), axis=0, keepdims=True))
            masks = jnp.where(rows == i * SIDE + j, mask, masks)
    before = lax.broadcasted_iota(jnp.int32, (128, 128), 0) < lax.broadcasted_iota(
        jnp.int32, (128, 128), 1
    )
    rank = jnp.dot(
        masks.astype(jnp.bfloat16),
        before.astype(jnp.float32).astype(jnp.bfloat16),
        preferred_element_type=jnp.float32,
    )
    rank = jnp.where(masks > 0.5, rank, -1.0)
    slot = lax.broadcasted_iota(jnp.int32, (SLOTS, 128), 0).astype(jnp.float32)
    for i in range(SIDE):
        for j in range(SIDE):
            n = i * SIDE + j
            pick = jnp.where(slot == rank[n : n + 1, :], 1.0, 0.0)
            pick_ref[i, j * SLOTS : (j + 1) * SLOTS, :] = pick.astype(jnp.bfloat16)
            put_ref[i, j, :, :] = pick.T.astype(jnp.bfloat16)
            column = jnp.sum(pick * weights[n], axis=1, keepdims=True)
            weight_ref[i, j * SLOTS : (j + 1) * SLOTS, :] = jnp.broadcast_to(column, (SLOTS, 128))


def route(dest, metas):
    return pl.pallas_call(
        route_kernel,
        out_shape=(
            jax.ShapeDtypeStruct((SIDE, SIDE * SLOTS, 128), jnp.bfloat16),
            jax.ShapeDtypeStruct((SIDE, SIDE, 128, SLOTS), jnp.bfloat16),
            jax.ShapeDtypeStruct((SIDE, SIDE * SLOTS, 128), jnp.float32),
        ),
        in_specs=[pl.BlockSpec(memory_space=pltpu.SMEM)]
        + [pl.BlockSpec(memory_space=pltpu.VMEM)] * 4,
        out_specs=(pl.BlockSpec(memory_space=pltpu.VMEM),) * 3,
        cost_estimate=FREE,
        name="route",
    )(dest, *metas)


def select_kernel(scaled, pick_ref, weight_ref, b0, b1, b2, b3, o0, o1, o2, o3):
    outs = (o0, o1, o2, o3)
    for i, block in enumerate((b0, b1, b2, b3)):
        rows = jnp.dot(pick_ref[i], block[...], preferred_element_type=jnp.float32)
        if scaled:
            rows = rows * weight_ref[i][:, 0:1]
        rows = rows.astype(jnp.bfloat16)
        for j in range(SIDE):
            outs[j][i, :, :] = rows[j * SLOTS : (j + 1) * SLOTS, :]


def select(pick, weight, blocks, scaled):
    width = blocks[0].shape[1]
    tile = 512
    return pl.pallas_call(
        functools.partial(select_kernel, scaled),
        out_shape=(jax.ShapeDtypeStruct((SIDE, SLOTS, width), jnp.bfloat16),) * SIDE,
        grid=(width // tile,),
        in_specs=[
            pl.BlockSpec((SIDE, SIDE * SLOTS, 128), lambda c: (0, 0, 0)),
            pl.BlockSpec((SIDE, SIDE * SLOTS, 128), lambda c: (0, 0, 0)),
        ]
        + [pl.BlockSpec((128, tile), lambda c: (0, c))] * SIDE,
        out_specs=(pl.BlockSpec((SIDE, SLOTS, tile), lambda c: (0, 0, c)),) * SIDE,
        compiler_params=PARAMS,
        cost_estimate=FREE,
        name="select_scaled" if scaled else "select",
    )(pick, weight, *blocks)


def combine_kernel(put_ref, r0, r1, r2, r3, o0, o1, o2, o3):
    returned = (r0, r1, r2, r3)
    for i, out in enumerate((o0, o1, o2, o3)):
        total = jnp.dot(put_ref[i, 0], r0[i], preferred_element_type=jnp.float32)
        for j in range(1, SIDE):
            total += jnp.dot(put_ref[i, j], returned[j][i], preferred_element_type=jnp.float32)
        out[...] = total.astype(jnp.bfloat16)


def combine(put, returned):
    width = returned[0].shape[2]
    tile = 512
    return pl.pallas_call(
        combine_kernel,
        out_shape=(jax.ShapeDtypeStruct((128, width), jnp.bfloat16),) * SIDE,
        grid=(width // tile,),
        in_specs=[pl.BlockSpec((SIDE, SIDE, 128, SLOTS), lambda c: (0, 0, 0, 0))]
        + [pl.BlockSpec((SIDE, SLOTS, tile), lambda c: (0, 0, c))] * SIDE,
        out_specs=(pl.BlockSpec((128, tile), lambda c: (0, c)),) * SIDE,
        compiler_params=PARAMS,
        cost_estimate=FREE,
        name="combine",
    )(put, *returned)


TILE = 512
ROWS = SIDE * SLOTS
ROWS_FIRST = (((0,), (0,)), ((), ()))
COLS_LAST = (((1,), (1,)), ((), ()))


def dot(a, b, dims=(((1,), (0,)), ((), ()))):
    return lax.dot_general(a, b, dims, preferred_element_type=jnp.float32)


def pre_kernel(n, *refs):
    xs, up, pres, acts = refs[:n], refs[n], refs[n + 1 : 2 * n + 1], refs[2 * n + 1 :]
    step = pl.program_id(0)
    for x, pre, act in zip(xs, pres, acts):
        part = dot(x[...], up[...])

        @pl.when(step == 0)
        def _():
            pre[...] = part

        @pl.when(step > 0)
        def _():
            pre[...] += part

        @pl.when(step == pl.num_programs(0) - 1)
        def _():
            value = pre[...]
            active = value * jax.nn.sigmoid(value)
            act[...] = active.T.astype(jnp.bfloat16).reshape(act.shape)


def expert_pre(xs, up):
    n, (width, hidden) = len(xs), up.shape
    out = pl.pallas_call(
        functools.partial(pre_kernel, n),
        out_shape=(jax.ShapeDtypeStruct((ROWS, hidden), jnp.float32),) * n
        + (jax.ShapeDtypeStruct((8, hidden // 8, ROWS), jnp.bfloat16),) * n,
        grid=(width // TILE,),
        in_specs=[pl.BlockSpec((ROWS, TILE), lambda c: (0, c))] * n
        + [pl.BlockSpec((TILE, hidden), lambda c: (c, 0))],
        out_specs=(pl.BlockSpec((ROWS, hidden), lambda c: (0, 0)),) * n
        + (pl.BlockSpec((8, hidden // 8, ROWS), lambda c: (0, 0, 0)),) * n,
        compiler_params=PARAMS,
        cost_estimate=FREE,
        name="expert_pre",
    )(*xs, up)
    return list(zip(out[:n], out[n:]))


def back_kernel(n, *refs):
    gs, pres, down, up = refs[:n], refs[n : 2 * n], refs[2 * n], refs[2 * n + 1]
    grads, rows, back = refs[2 * n + 2 : 3 * n + 2], refs[3 * n + 2 : 4 * n + 2], refs[-1]
    step = pl.program_id(0)
    half = pl.num_programs(0) // 2

    @pl.when(step == 0)
    def _():
        for i in range(n):
            back[i] = dot(gs[i][...], down[...], COLS_LAST)

    @pl.when(jnp.logical_and(step > 0, step < half))
    def _():
        for i in range(n):
            back[i] += dot(gs[i][...], down[...], COLS_LAST)

    @pl.when(step == half - 1)
    def _():
        for i in range(n):
            value = pres[i][...]
            sigma = jax.nn.sigmoid(value)
            grad = back[i] * sigma * (1.0 + value * (1.0 - sigma))
            grads[i][...] = grad.astype(jnp.bfloat16)

    @pl.when(step >= half)
    def _():
        for i in range(n):
            rows[i][...] = dot(grads[i][...], up[...], COLS_LAST).astype(jnp.bfloat16)


def expert_back(gs, pres, down, up):
    n, (width, hidden) = len(gs), up.shape
    tiles = width // TILE
    out = pl.pallas_call(
        functools.partial(back_kernel, n),
        out_shape=(jax.ShapeDtypeStruct((ROWS, hidden), jnp.bfloat16),) * n
        + (jax.ShapeDtypeStruct((ROWS, width), jnp.bfloat16),) * n,
        grid=(2 * tiles,),
        in_specs=[pl.BlockSpec((ROWS, TILE), lambda c: (0, jnp.minimum(c, tiles - 1)))] * n
        + [pl.BlockSpec((ROWS, hidden), lambda c: (0, 0))] * n
        + [
            pl.BlockSpec((hidden, TILE), lambda c: (0, jnp.minimum(c, tiles - 1))),
            pl.BlockSpec((TILE, hidden), lambda c: (jnp.maximum(c - tiles, 0), 0)),
        ],
        out_specs=(pl.BlockSpec((ROWS, hidden), lambda c: (0, 0)),) * n
        + (pl.BlockSpec((ROWS, TILE), lambda c: (0, jnp.maximum(c - tiles, 0))),) * n,
        scratch_shapes=[pltpu.VMEM((n, ROWS, hidden), jnp.float32)],
        compiler_params=PARAMS,
        cost_estimate=FREE,
        name="expert_back",
    )(*gs, *pres, down, up)
    return list(zip(out[:n], out[n:]))


def up_kernel(kept, idx, *refs):
    xs, grads = refs[:SIDE], refs[SIDE : 2 * SIDE]
    total = sum(dot(x[...], p[...], ROWS_FIRST) for x, p in zip(xs, grads))
    if not kept:
        refs[-1][0] = total.astype(jnp.bfloat16)
        return
    total += refs[2 * SIDE][0].astype(jnp.float32)
    for k, out in enumerate(refs[2 * SIDE + 1 :]):

        @pl.when(pl.program_id(0) == k)
        def _():
            out[...] = total.astype(jnp.bfloat16)


def up_part(idx, xs, grads, received=None):
    hidden = grads[0].shape[1]
    kept = received is not None
    block = xs[0].shape[1] // 8
    slab = pl.BlockSpec((1, block, hidden), lambda s, idx: (s, 0, 0))
    if kept:
        shape = (jax.ShapeDtypeStruct((block, hidden), jnp.bfloat16),) * SIDE
        out_specs = (pl.BlockSpec((block, hidden), lambda s, idx: (0, 0)),) * SIDE
    else:
        shape = jax.ShapeDtypeStruct((SIDE, block, hidden), jnp.bfloat16)
        out_specs = slab
    return pl.pallas_call(
        functools.partial(up_kernel, kept),
        out_shape=shape,
        grid_spec=pltpu.PrefetchScalarGridSpec(
            num_scalar_prefetch=1,
            grid=(SIDE,),
            in_specs=[pl.BlockSpec((ROWS, block), lambda s, idx: (0, idx[s]))] * SIDE
            + [pl.BlockSpec((ROWS, hidden), lambda s, idx: (0, 0))] * SIDE
            + ([slab] if kept else []),
            out_specs=out_specs,
        ),
        compiler_params=PARAMS,
        cost_estimate=FREE,
        name="up_keep" if kept else "up_give",
    )(idx, *xs, *grads, *([received] if kept else []))


def down_kernel(kept, idx, *refs):
    acts, gs, lhs = refs[:SIDE], refs[SIDE : 2 * SIDE], refs[-1]
    part = acts[0].shape[1]

    @pl.when(pl.program_id(0) == 0)
    def _():
        for j, act in enumerate(acts):
            for s in range(SIDE):
                lhs[j, s * part : (s + 1) * part, :] = act[idx[s]]

    total = sum(dot(lhs[j], g[...]) for j, g in enumerate(gs))
    for s in range(SIDE):
        piece = total[s * part : (s + 1) * part, :]
        if kept:
            piece += refs[2 * SIDE][s].astype(jnp.float32)
            refs[2 * SIDE + 1 + s][...] = piece.astype(jnp.bfloat16)
        else:
            refs[2 * SIDE][s] = piece.astype(jnp.bfloat16)


def down_part(idx, acts, gs, received=None):
    kept = received is not None
    part, width = acts[0].shape[1], gs[0].shape[1]
    slab = pl.BlockSpec((SIDE, part, TILE), lambda c, idx: (0, 0, c))
    if kept:
        shape = (jax.ShapeDtypeStruct((part, width), jnp.bfloat16),) * SIDE
        out_specs = (pl.BlockSpec((part, TILE), lambda c, idx: (0, c)),) * SIDE
    else:
        shape = jax.ShapeDtypeStruct((SIDE, part, width), jnp.bfloat16)
        out_specs = slab
    return pl.pallas_call(
        functools.partial(down_kernel, kept),
        out_shape=shape,
        grid_spec=pltpu.PrefetchScalarGridSpec(
            num_scalar_prefetch=1,
            grid=(width // TILE,),
            in_specs=[pl.BlockSpec((8, part, ROWS), lambda c, idx: (0, 0, 0))] * SIDE
            + [pl.BlockSpec((ROWS, TILE), lambda c, idx: (0, c))] * SIDE
            + ([slab] if kept else []),
            out_specs=out_specs,
            scratch_shapes=[pltpu.VMEM((SIDE, SIDE * part, ROWS), jnp.bfloat16)],
        ),
        compiler_params=PARAMS,
        cost_estimate=FREE,
        name="down_keep" if kept else "down_give",
    )(idx, *acts, *gs, *([received] if kept else []))


def swap_cores(value):
    return lax.ppermute(value, "dp", [(d, d ^ 1) for d in range(8)])


def send_z(value, shift):
    pairs = [(z * 2 + c, (z + shift) % SIDE * 2 + c) for z in range(SIDE) for c in range(2)]
    return value if shift == 0 else lax.ppermute(value, "dp", pairs)


def after(value, *earlier):
    return lax.optimization_barrier((value, *earlier))[0]


def body(tokens, cotangent, expert_ids, route_weight, up_weight, down_weight):
    width = tokens.shape[1]
    up_matrix = up_weight[0]
    down_matrix = down_weight[0]
    dp = lax.axis_index("dp")
    core, z = dp & 1, dp >> 1
    place = lax.axis_index("expert")
    y, x = place >> 2, place & 3
    shifts = jnp.array(OFFSETS, jnp.int32)
    dest = jnp.where(core == 1, y * SIDE + ((x + shifts) & 3), ((y + shifts) & 3) * SIDE + x)
    keep = ((z + shifts) & 3) * 2 + core
    give = ((z + shifts) & 3) * 2 + 1 - core
    meta = jnp.concatenate([expert_ids.astype(jnp.float32).T, route_weight.T], axis=0)

    metas = [send(meta, True, o) for o in OFFSETS]
    token_blocks = [send(tokens, True, o) for o in OFFSETS]
    pick, put, weight = route(dest, metas)
    cotangent = after(cotangent, *token_blocks)
    cot_blocks = [send(cotangent, True, o) for o in OFFSETS]

    out_x = select(pick, weight, token_blocks, False)
    rx = [None] * SIDE
    rx[0], rx[1], rx[2] = (send(out_x[i], False, OFFSETS[i]) for i in range(3))
    rx[3] = send(after(out_x[3], rx[1], rx[2]), False, OFFSETS[3])
    out_g = select(pick, weight, cot_blocks, True)
    rg = [None] * SIDE
    rg[0] = out_g[0]
    rg[1], rg[2] = (send(after(out_g[i], rx[1], rx[2]), False, OFFSETS[i]) for i in (1, 2))
    rg[3] = send(after(out_g[3], rg[1], rg[2], rx[3]), False, OFFSETS[3])
    rx = [r.reshape(ROWS, width) for r in rx]
    rg = [r.reshape(ROWS, width) for r in rg]

    pre, back = [], []
    for group in ((0,), (1, 2), (3,)):
        pre += expert_pre([rx[i] for i in group], up_matrix)
    for group in ((0,), (1, 2), (3,)):
        back += expert_back(
            [rg[i] for i in group], [pre[i][0] for i in group], down_matrix, up_matrix
        )
    acts = [p[1] for p in pre]
    grads = [b[0] for b in back]
    row_grads = [b[1].reshape(SIDE, SLOTS, width) for b in back]
    returned = [send(r, False, -o) for r, o in zip(row_grads, OFFSETS)]

    acts[3] = after(acts[3], row_grads[3])
    down_give = down_part(give, acts, rg)
    up_give = up_part(give, rx, grads)
    down_keep = down_part(keep, acts, rg, swap_cores(down_give))
    up_keep = up_part(keep, rx, grads, swap_cores(up_give))
    down_sum = [send_z(p, o).astype(jnp.float32) for p, o in zip(down_keep, OFFSETS)]
    up_sum = [send_z(p, o).astype(jnp.float32) for p, o in zip(up_keep, OFFSETS)]

    parts = combine(put, returned)
    parts = [send(p, True, -o) for p, o in zip(parts, OFFSETS)]
    token_grad = sum(p.astype(jnp.float32) for p in parts).astype(jnp.bfloat16)
    return token_grad, sum(up_sum)[None], sum(down_sum)[None]


def solution(mesh):
    rows = P(("dp", "expert"), None)
    weights = P("expert", None, None)
    return jax.shard_map(
        body,
        mesh=mesh,
        in_specs=(rows, rows, rows, rows, weights, weights),
        out_specs=(rows, P("expert", "dp", None), P("expert", "dp", None)),
        check_vma=False,
    )
```

time: 360 us -> 380 us (1.056)
  Pallas kernels: 58.4 us -> 131 us
  matrix products: 51.6 us -> 0 us
  waiting for transfers between devices: 180 us -> 142 us
  starting transfers between devices: 38.2 us -> 63.8 us
  local copies, waits for them, and re-layouts: 8 us -> 30.4 us
  between operations: 14.3 us -> 1.09 us
    pallas_call x2 -> x10, Pallas kernels: 34 us -> 107 us  [the longest x3 45.3 us: expert_back(): pl.pallas_call(functools.partial(back_kernel, n), out_shape=(jax.ShapeDty...]
    ppermute x21, waiting for transfers between devices: 180 us -> 110 us  [send(): lax.ppermute(value, BOTH, ring(first, shift))]
    dot_general x12 -> x0, matrix products: 51.6 us -> none  [the longest x4 19.6 us: body(): lax.dot_general(rg, down_matrix, (((1,), (1,)), ((), ())), preferred_elem...]
    ppermute x0 -> x8, waiting for transfers between devices: none -> 31.6 us  [the longest x6 31.6 us: send_z(): return value if shift == 0 else lax.ppermute(value, 'dp', pairs)]
    ppermute x0 -> x8, starting transfers between devices: none -> 28.4 us  [the longest x6 27.9 us: send_z(): return value if shift == 0 else lax.ppermute(value, 'dp', pairs)]
    unnamed x52 -> x134, local copies, waits for them, and re-layouts: 8 us -> 30.4 us
  transfers between devices with their start and end apart: 23 -> 29, of which waited for: 11 -> 10; matrix products, arithmetic and copies ran while one was open for 16% -> 2% of each run, Pallas kernels for 10% -> 33%
where the time goes in v2:
time: 380 us; the launch traced here: 377 us
  waiting for transfers between devices  142 us (37%)
  Pallas kernels  131 us (34%)
  starting transfers between devices  63.8 us (17%)
  local copies, waits for them, and re-layouts  30.4 us (8%)
  other arithmetic  9.1 us (2%)
    ppermute x21, waiting for transfers between devices, send(): lax.ppermute(value, BOTH, ring(first, shift))  110 us
    pallas_call x3, Pallas kernels, expert_back(): pl.pallas_call(functools.partial(back_kernel, n), out_shape=(jax.ShapeDty...  45.3 us
    ppermute x21, starting transfers between devices, send(): lax.ppermute(value, BOTH, ring(first, shift))  35.3 us
    ppermute x6, waiting for transfers between devices, send_z(): return value if shift == 0 else lax.ppermute(value, 'dp', pairs)  31.6 us
    unnamed x134, local copies, waits for them, and re-layouts  30.4 us
    ppermute x6, starting transfers between devices, send_z(): return value if shift == 0 else lax.ppermute(value, 'dp', pairs)  27.9 us
    pallas_call x2, Pallas kernels, down_part(): pl.pallas_call(functools.partial(down_kernel, kept), out_shape=shape, gri...  22.8 us
    pallas_call x2, Pallas kernels, up_part(): pl.pallas_call(functools.partial(up_kernel, kept), out_shape=shape, grid_...  19.9 us
  transfers between devices with their start and end apart: 29, of which 10 were waited for; matrix products, arithmetic and copies ran while one was open for 2% of the time, Pallas kernels for 33%

profile of v2, /device:TPU:0, one launch (start us, length us, event | category | flops | bytes accessed | tf_op | source)
XLA Modules:
  0.0 377.4 jit_solution(6770243248932434965)
XLA Ops:
  10.4 15.7 %collective-permute-done.m1 = f32[16,128]{1,0:T(8,128)S(1)} collective-permute-done((f32[16,128]{1,0:T(8,128)S(1)}, f32[16,128]{1,0:T(8,128)S(1)}, u32[]{:S(2)}, u32[]{:S(2)}) %collective-permute-start) | collective-permute-done | bytes 8224 | tf_op jit(solution)/shard_map/ppermute | solution.py:32
  26.2 4.0 %collective-permute-start.2 = (f32[16,128]{1,0:T(8,128)S(1)}, f32[16,128]{1,0:T(8,128)S(1)}, u32[]{:S(2)}, u32[]{:S(2)}) collective-permute-start(f32[16,128]{1,0:T(8,128)S(1)} %pad_maximum_fusion.m0), channel_id=1, source_target_pairs={{0,2},{1,3},{2,0},{3,1},{4,6},{5,7},{6,4},{7,5},{8,10},{9,11},{10,... | collective-permute-start | bytes 24584 | tf_op jit(solution)/shard_map/ppermute | solution.py:32
  37.8 6.3 %select.1 = (bf16[4,72,4096]{2,1,0:T(8,128)(2,1)S(1)}, bf16[4,72,4096]{2,1,0:T(8,128)(2,1)}, bf16[4,72,4096]{2,1,0:T(8,128)(2,1)}, bf16[4,72,4096]{2,1,0:T(8,128)(2,1)S(1)}) custom-call(bf16[4,288,128]{2,1,0:T(8,128)(2,1)S(1)} %copy-done.44, f32[4,288,128]{2,1,0:T(8,128)S(1)} %copy-done.30, bf16[128,4096]{1,0:T(8,128)(2,1)S(1)} %copy-done.45, ...), custom_call_target="tpu_custom_call" | custom-call | flops 1 | bytes 1 | tf_op jit(solution)/shard_map/select/pallas_call | solution.py:96
  54.1 22.0 %collective-permute-done.6.b1 = bf16[128,4096]{1,0:T(8,128)(2,1)S(1)} collective-permute-done((bf16[128,4096]{1,0:T(8,128)(2,1)}, bf16[128,4096]{1,0:T(8,128)(2,1)S(1)}, u32[]{:S(2)}, u32[]{:S(2)}) %collective-permute-start.6) | collective-permute-done | bytes 1048608 | tf_op jit(solution)/shard_map/ppermute | solution.py:32
  76.9 20.4 %collective-permute-done.8.b3 = bf16[128,4096]{1,0:T(8,128)(2,1)S(1)} collective-permute-done((bf16[128,4096]{1,0:T(8,128)(2,1)}, bf16[128,4096]{1,0:T(8,128)(2,1)S(1)}, u32[]{:S(2)}, u32[]{:S(2)}) %collective-permute-start.8) | collective-permute-done | bytes 1048608 | tf_op jit(solution)/shard_map/ppermute | solution.py:32
  98.5 5.9 %select_scaled.1 = (bf16[4,72,4096]{2,1,0:T(8,128)(2,1)S(1)}, bf16[4,72,4096]{2,1,0:T(8,128)(2,1)S(1)}, bf16[4,72,4096]{2,1,0:T(8,128)(2,1)S(1)}, bf16[4,72,4096]{2,1,0:T(8,128)(2,1)}) custom-call(bf16[4,288,128]{2,1,0:T(8,128)(2,1)S(1)} %copy-done.44, f32[4,288,128]{2,1,0:T(8,128)S(1)} %copy-done.30, bf16[128,4096]{1,0:T(8,128)(2,1)S(1)} %copy-done.46, ...), custom_call_target="tpu_custom_call" | custom-call | flops 1 | bytes 1 | tf_op jit(solution)/shard_map/select_scaled/pallas_call | solution.py:96
  108.7 3.2 collective-permute-start.15
  114.0 25.5 %collective-permute-done.15 = bf16[4,72,4096]{2,1,0:T(8,128)(2,1)S(1)} collective-permute-done((bf16[4,72,4096]{2,1,0:T(8,128)(2,1)}, bf16[4,72,4096]{2,1,0:T(8,128)(2,1)S(1)}, u32[]{:S(2)}, u32[]{:S(2)}) %collective-permute-start.15) | collective-permute-done | bytes 2359328 | tf_op jit(solution)/shard_map/ppermute | solution.py:32
  139.5 25.5 %collective-permute-done.12 = bf16[4,72,4096]{2,1,0:T(8,128)(2,1)S(1)} collective-permute-done((bf16[4,72,4096]{2,1,0:T(8,128)(2,1)}, bf16[4,72,4096]{2,1,0:T(8,128)(2,1)S(1)}, u32[]{:S(2)}, u32[]{:S(2)}) %collective-permute-start.12) | collective-permute-done | bytes 2359328 | tf_op jit(solution)/shard_map/ppermute | solution.py:32
  167.8 10.5 %expert_pre.4 = (f32[288,768]{1,0:T(8,128)S(1)}, f32[288,768]{1,0:T(8,128)S(1)}, bf16[8,96,288]{2,1,0:T(8,128)(2,1)S(1)}, bf16[8,96,288]{2,1,0:T(8,128)(2,1)S(1)}) custom-call(bf16[288,4096]{1,0:T(8,128)(2,1)} %bitcast.9.refs_0_.refs_1_, bf16[288,4096]{1,0:T(8,128)(2,1)S(1)} %bitcast.43, bf16[4096,768]{1,0:T(8,128)(2,1)S(1)} %bitcast.24), custom_call_target="tpu_custom_call" | custom-call | flops 1 | bytes 1 | tf_op jit(solution)/shard_map/expert_pre/pallas_call | solution.py:170
  181.9 4.3 %expert_pre.5 = (f32[288,768]{1,0:T(8,128)S(1)}, bf16[8,96,288]{2,1,0:T(8,128)(2,1)S(1)}) custom-call(bf16[288,4096]{1,0:T(8,128)(2,1)S(1)} %bitcast.46, bf16[4096,768]{1,0:T(8,128)(2,1)S(1)} %bitcast.25), custom_call_target="tpu_custom_call" | custom-call | flops 1 | bytes 1 | tf_op jit(solution)/shard_map/expert_pre/pallas_call | solution.py:170
  189.4 18.4 %expert_back.4 = (bf16[288,768]{1,0:T(8,128)(2,1)S(1)}, bf16[288,768]{1,0:T(8,128)(2,1)S(1)}, bf16[288,4096]{1,0:T(8,128)(2,1)}, bf16[288,4096]{1,0:T(8,128)(2,1)}) custom-call(bf16[288,4096]{1,0:T(8,128)(2,1)S(1)} %bitcast.37, bf16[288,4096]{1,0:T(8,128)(2,1)S(1)} %bitcast.34, f32[288,768]{1,0:T(8,128)S(1)} %get-tuple-element.62.refs_2_, ...), custom_call_target="tpu_custom_call" | custom-call | flops 1 | bytes 1 | tf_op jit(solution)/shard_map/expert_back/pallas_call | solution.py:219
  211.9 14.6 %expert_back.5 = (bf16[288,768]{1,0:T(8,128)(2,1)S(1)}, bf16[288,4096]{1,0:T(8,128)(2,1)}) custom-call(bf16[288,4096]{1,0:T(8,128)(2,1)} %bitcast.13.refs_0_.refs_7_, f32[288,768]{1,0:T(8,128)S(1)} %copy-done.52, bf16[768,4096]{1,0:T(8,128)(2,1)S(1)} %bitcast.32, bf16[4096,768]{1,0:T(8,128)(2,1)} %bitcast.22), custom_call_target="tpu_custom_call" | custom-call | flops 1 | bytes 1 | tf_op jit(solution)/shard_map/expert_back/pallas_call | solution.py:219
  227.3 4.3 %expert_pre.3 = (f32[288,768]{1,0:T(8,128)S(1)}, bf16[8,96,288]{2,1,0:T(8,128)(2,1)S(1)}) custom-call(bf16[288,4096]{1,0:T(8,128)(2,1)S(1)} %bitcast.40, bf16[4096,768]{1,0:T(8,128)(2,1)S(1)} %bitcast.28), custom_call_target="tpu_custom_call" | custom-call | flops 1 | bytes 1 | tf_op jit(solution)/shard_map/expert_pre/pallas_call | solution.py:170
  233.6 12.4 %expert_back.3 = (bf16[288,768]{1,0:T(8,128)(2,1)S(1)}, bf16[288,4096]{1,0:T(8,128)(2,1)S(1)}) custom-call(bf16[288,4096]{1,0:T(8,128)(2,1)S(1)} %bitcast.49, f32[288,768]{1,0:T(8,128)S(1)} %get-tuple-element.54.refs_1_, bf16[768,4096]{1,0:T(8,128)(2,1)S(1)} %bitcast.33, bf16[4096,768]{1,0:T(8,128)(2,1)} %bitcast.23), custom_call_target="tpu_custom_call" | custom-call | flops 1 | bytes 1 | tf_op jit(solution)/shard_map/expert_back/pallas_call | solution.py:219
  247.5 11.3 %down_give.1 = bf16[4,96,4096]{2,1,0:T(8,128)(2,1)} custom-call(s32[4]{0:T(128)S(1)} %get-tuple-element.93.idx, bf16[8,96,288]{2,1,0:T(8,128)(2,1)S(1)} %get-tuple-element.84.refs_0_, bf16[8,96,288]{2,1,0:T(8,128)(2,1)S(1)} %copy-done.20, bf16[8,96,288]{2,1,0:T(8,128)(2,1)S(1)} %copy-done.23, bf16[8,96,288]{2,1,0:T(8,128)(2,1)S(1)} %copy-done.26, ...), custom_call_target="tpu_custom_call" | custom-call | flops 1 | bytes 1 | tf_op jit(solution)/shard_map/down_give/pallas_call | solution.py:312
  258.9 10.0 %up_give.1 = bf16[4,512,768]{2,1,0:T(8,128)(2,1)} custom-call(s32[4]{0:T(128)S(1)} %get-tuple-element.93.idx, bf16[288,4096]{1,0:T(8,128)(2,1)S(1)} %bitcast.41, bf16[288,4096]{1,0:T(8,128)(2,1)} %bitcast.9.refs_0_.refs_1_, bf16[288,4096]{1,0:T(8,128)(2,1)S(1)} %bitcast.44, bf16[288,4096]{1,0:T(8,128)(2,1)S(1)} %bitcast.47, ...), custom_call_target="tpu_custom_call" | custom-call | flops 1 | bytes 1 | tf_op jit(solution)/shard_map/up_give/pallas_call | solution.py:265
  271.1 9.7 %combine.1 = (bf16[128,4096]{1,0:T(8,128)(2,1)S(1)}, bf16[128,4096]{1,0:T(8,128)(2,1)}, bf16[128,4096]{1,0:T(8,128)(2,1)}, bf16[128,4096]{1,0:T(8,128)(2,1)}) custom-call(bf16[4,4,128,72]{3,2,1,0:T(8,128)(2,1)S(1)} %copy-done.53, bf16[4,72,4096]{2,1,0:T(8,128)(2,1)S(1)} %bitcast.52, bf16[4,72,4096]{2,1,0:T(8,128)(2,1)} %collective-permute-done.13.r1, ...), custom_call_target="tpu_custom_call" | custom-call | flops 1 | bytes 1 | tf_op jit(solution)/shard_map/combine/pallas_call | solution.py:124
  289.0 11.5 %down_keep.1 = (bf16[96,4096]{1,0:T(8,128)(2,1)S(1)}, bf16[96,4096]{1,0:T(8,128)(2,1)}, bf16[96,4096]{1,0:T(8,128)(2,1)}, bf16[96,4096]{1,0:T(8,128)(2,1)S(1)}) custom-call(s32[4]{0:T(128)S(1)} %get-tuple-element.95.idx, bf16[8,96,288]{2,1,0:T(8,128)(2,1)S(1)} %copy-done.29, bf16[8,96,288]{2,1,0:T(8,128)(2,1)S(1)} %copy-done.21, ...), custom_call_target="tpu_custom_call" | custom-call | flops 1 | bytes 1 | tf_op jit(solution)/shard_map/down_keep/pallas_call | solution.py:312
  305.6 9.8 %up_keep.1 = (bf16[512,768]{1,0:T(8,128)(2,1)S(1)}, bf16[512,768]{1,0:T(8,128)(2,1)S(1)}, bf16[512,768]{1,0:T(8,128)(2,1)S(1)}, bf16[512,768]{1,0:T(8,128)(2,1)S(1)}) custom-call(s32[4]{0:T(128)S(1)} %get-tuple-element.95.idx, bf16[288,4096]{1,0:T(8,128)(2,1)S(1)} %bitcast.42, bf16[288,4096]{1,0:T(8,128)(2,1)} %bitcast.9.refs_0_.refs_1_, ...), custom_call_target="tpu_custom_call" | custom-call | flops 1 | bytes 1 | tf_op jit(solution)/shard_map/up_keep/pallas_call | solution.py:265
  320.6 3.5 add_convert_fusion
  324.0 18.7 %collective-permute-start.24 = (bf16[512,768]{1,0:T(8,128)(2,1)S(1)}, bf16[512,768]{1,0:T(8,128)(2,1)S(1)}, u32[]{:S(2)}, u32[]{:S(2)}) collective-permute-start(bf16[512,768]{1,0:T(8,128)(2,1)S(1)} %get-tuple-element.83), channel_id=1, source_target_pairs={{0,64},{16,80},{32,96},{48,112},{64,0},{80,16},{96,32},{112,48},{1... | collective-permute-start | bytes 2359304 | tf_op jit(solution)/shard_map/ppermute | solution.py:336
  344.3 13.4 %collective-permute-done.22 = bf16[512,768]{1,0:T(8,128)(2,1)S(1)} collective-permute-done((bf16[512,768]{1,0:T(8,128)(2,1)S(1)}, bf16[512,768]{1,0:T(8,128)(2,1)S(1)}, u32[]{:S(2)}, u32[]{:S(2)}) %collective-permute-start.22) | collective-permute-done | bytes 786464 | tf_op jit(solution)/shard_map/ppermute | solution.py:336
  357.7 16.3 %collective-permute-done.23 = bf16[512,768]{1,0:T(8,128)(2,1)S(1)} collective-permute-done((bf16[512,768]{1,0:T(8,128)(2,1)S(1)}, bf16[512,768]{1,0:T(8,128)(2,1)S(1)}, u32[]{:S(2)}, u32[]{:S(2)}) %collective-permute-start.23) | collective-permute-done | bytes 786464 | tf_op jit(solution)/shard_map/ppermute | solution.py:336
  (190 shorter events, 79.1 us)
Async XLA Ops:
  0.6 33.9 %collective-permute-start.3 = (bf16[128,4096]{1,0:T(8,128)(2,1)}, bf16[128,4096]{1,0:T(8,128)(2,1)S(1)}, u32[]{:S(2)}, u32[]{:S(2)}) collective-permute-start(bf16[128,4096]{1,0:T(8,128)(2,1)} %b0.2), channel_id=1, source_target_pairs={{0,1},{1,2},{2,3},{3,0},{4,5},{5,6},{6,7},{7,4},{8,9},{9,10},{10,1... | collective-permute-start | bytes 3145736 | tf_op jit(solution)/shard_map/ppermute | solution.py:32
  2.3 32.2 %collective-permute-start.4 = (bf16[128,4096]{1,0:T(8,128)(2,1)}, bf16[128,4096]{1,0:T(8,128)(2,1)S(1)}, u32[]{:S(2)}, u32[]{:S(2)}) collective-permute-start(bf16[128,4096]{1,0:T(8,128)(2,1)} %b0.2), channel_id=1, source_target_pairs={{0,3},{1,0},{2,1},{3,2},{4,7},{5,4},{6,5},{7,6},{8,11},{9,8},{10,9... | collective-permute-start | bytes 3145736 | tf_op jit(solution)/shard_map/ppermute | solution.py:32
  3.9 30.6 %collective-permute-start.5 = (bf16[128,4096]{1,0:T(8,128)(2,1)}, bf16[128,4096]{1,0:T(8,128)(2,1)S(1)}, u32[]{:S(2)}, u32[]{:S(2)}) collective-permute-start(bf16[128,4096]{1,0:T(8,128)(2,1)} %b0.2), channel_id=1, source_target_pairs={{0,2},{1,3},{2,0},{3,1},{4,6},{5,7},{6,4},{7,5},{8,10},{9,11},{10,... | collective-permute-start | bytes 3145736 | tf_op jit(solution)/shard_map/ppermute | solution.py:32
  45.5 63.2 %collective-permute-start.10 = (bf16[4,72,4096]{2,1,0:T(8,128)(2,1)}, bf16[4,72,4096]{2,1,0:T(8,128)(2,1)S(1)}, u32[]{:S(2)}, u32[]{:S(2)}) collective-permute-start(bf16[4,72,4096]{2,1,0:T(8,128)(2,1)} %get-tuple-element.58), channel_id=1, source_target_pairs={{0,12},{1,13},{2,14},{3,15},{4,0},{5,1},{6,2},{7,3},{8,4},{9,5},{1... | collective-permute-start | bytes 7077896 | tf_op jit(solution)/shard_map/ppermute | solution.py:32
  48.5 60.2 %collective-permute-start.9 = (bf16[4,72,4096]{2,1,0:T(8,128)(2,1)}, bf16[4,72,4096]{2,1,0:T(8,128)(2,1)}, u32[]{:S(2)}, u32[]{:S(2)}) collective-permute-start(bf16[4,72,4096]{2,1,0:T(8,128)(2,1)} %get-tuple-element.57), channel_id=1, source_target_pairs={{0,4},{1,5},{2,6},{3,7},{4,8},{5,9},{6,10},{7,11},{8,12},{9,13},{1... | collective-permute-start | bytes 7077896 | tf_op jit(solution)/shard_map/ppermute | solution.py:32
  48.5 27.6 %collective-permute-start.6 = (bf16[128,4096]{1,0:T(8,128)(2,1)}, bf16[128,4096]{1,0:T(8,128)(2,1)S(1)}, u32[]{:S(2)}, u32[]{:S(2)}) collective-permute-start(bf16[128,4096]{1,0:T(8,128)(2,1)} %b0.1), channel_id=1, source_target_pairs={{0,1},{1,2},{2,3},{3,0},{4,5},{5,6},{6,7},{7,4},{8,9},{9,10},{10,1... | collective-permute-start | bytes 3145736 | tf_op jit(solution)/shard_map/ppermute | solution.py:32
  51.8 45.5 %collective-permute-start.8 = (bf16[128,4096]{1,0:T(8,128)(2,1)}, bf16[128,4096]{1,0:T(8,128)(2,1)S(1)}, u32[]{:S(2)}, u32[]{:S(2)}) collective-permute-start(bf16[128,4096]{1,0:T(8,128)(2,1)} %b0.1), channel_id=1, source_target_pairs={{0,2},{1,3},{2,0},{3,1},{4,6},{5,7},{6,4},{7,5},{8,10},{9,11},{10,... | collective-permute-start | bytes 3145736 | tf_op jit(solution)/shard_map/ppermute | solution.py:32
  108.7 30.7 %collective-permute-start.15 = (bf16[4,72,4096]{2,1,0:T(8,128)(2,1)}, bf16[4,72,4096]{2,1,0:T(8,128)(2,1)S(1)}, u32[]{:S(2)}, u32[]{:S(2)}) collective-permute-start(bf16[4,72,4096]{2,1,0:T(8,128)(2,1)} %copy-done.54), channel_id=1, source_target_pairs={{0,8},{1,9},{2,10},{3,11},{4,12},{5,13},{6,14},{7,15},{8,0},{9,1},... | collective-permute-start | bytes 7077896 | tf_op jit(solution)/shard_map/ppermute | solution.py:32
  111.9 53.0 %collective-permute-start.12 = (bf16[4,72,4096]{2,1,0:T(8,128)(2,1)}, bf16[4,72,4096]{2,1,0:T(8,128)(2,1)S(1)}, u32[]{:S(2)}, u32[]{:S(2)}) collective-permute-start(bf16[4,72,4096]{2,1,0:T(8,128)(2,1)} %copy-done.56), channel_id=1, source_target_pairs={{0,12},{1,13},{2,14},{3,15},{4,0},{5,1},{6,2},{7,3},{8,4},{9,5},{1... | collective-permute-start | bytes 7077896 | tf_op jit(solution)/shard_map/ppermute | solution.py:32
  113.0 51.9 %collective-permute-start.11 = (bf16[4,72,4096]{2,1,0:T(8,128)(2,1)}, bf16[4,72,4096]{2,1,0:T(8,128)(2,1)S(1)}, u32[]{:S(2)}, u32[]{:S(2)}) collective-permute-start(bf16[4,72,4096]{2,1,0:T(8,128)(2,1)} %copy-done.55), channel_id=1, source_target_pairs={{0,4},{1,5},{2,6},{3,7},{4,8},{5,9},{6,10},{7,11},{8,12},{9,13},{1... | collective-permute-start | bytes 7077896 | tf_op jit(solution)/shard_map/ppermute | solution.py:32
  165.0 45.6 %collective-permute-start.16 = (bf16[4,72,4096]{2,1,0:T(8,128)(2,1)}, bf16[4,72,4096]{2,1,0:T(8,128)(2,1)}, u32[]{:S(2)}, u32[]{:S(2)}) collective-permute-start(bf16[4,72,4096]{2,1,0:T(8,128)(2,1)} %get-tuple-element.69), channel_id=1, source_target_pairs={{0,8},{1,9},{2,10},{3,11},{4,12},{5,13},{6,14},{7,15},{8,0},{9,1},... | collective-permute-start | bytes 7077896 | tf_op jit(solution)/shard_map/ppermute | solution.py:32
  208.5 60.9 %collective-permute-start.13 = (bf16[4,72,4096]{2,1,0:T(8,128)(2,1)}, bf16[4,72,4096]{2,1,0:T(8,128)(2,1)}, u32[]{:S(2)}, u32[]{:S(2)}) collective-permute-start(bf16[4,72,4096]{2,1,0:T(8,128)(2,1)} %bitcast.11), channel_id=1, source_target_pairs={{0,12},{1,13},{2,14},{3,15},{4,0},{5,1},{6,2},{7,3},{8,4},{9,5},{1... | collective-permute-start | bytes 7077896 | tf_op jit(solution)/shard_map/ppermute | solution.py:32
  209.9 59.5 %collective-permute-start.14 = (bf16[4,72,4096]{2,1,0:T(8,128)(2,1)}, bf16[4,72,4096]{2,1,0:T(8,128)(2,1)}, u32[]{:S(2)}, u32[]{:S(2)}) collective-permute-start(bf16[4,72,4096]{2,1,0:T(8,128)(2,1)} %bitcast.12), channel_id=1, source_target_pairs={{0,4},{1,5},{2,6},{3,7},{4,8},{5,9},{6,10},{7,11},{8,12},{9,13},{1... | collective-permute-start | bytes 7077896 | tf_op jit(solution)/shard_map/ppermute | solution.py:32
  226.5 42.9 %collective-permute-start.17 = (bf16[4,72,4096]{2,1,0:T(8,128)(2,1)}, bf16[4,72,4096]{2,1,0:T(8,128)(2,1)}, u32[]{:S(2)}, u32[]{:S(2)}) collective-permute-start(bf16[4,72,4096]{2,1,0:T(8,128)(2,1)} %bitcast.15), channel_id=1, source_target_pairs={{0,8},{1,9},{2,10},{3,11},{4,12},{5,13},{6,14},{7,15},{8,0},{9,1},... | collective-permute-start | bytes 7077896 | tf_op jit(solution)/shard_map/ppermute | solution.py:32
  258.8 26.4 %collective-permute-start.25 = (bf16[4,96,4096]{2,1,0:T(8,128)(2,1)}, bf16[4,96,4096]{2,1,0:T(8,128)(2,1)}, u32[]{:S(2)}, u32[]{:S(2)}) collective-permute-start(bf16[4,96,4096]{2,1,0:T(8,128)(2,1)} %down_give.1), channel_id=1, source_target_pairs={{0,16},{16,0},{32,48},{48,32},{64,80},{80,64},{96,112},{112,96},{1... | collective-permute-start | bytes 9437192 | tf_op jit(solution)/shard_map/ppermute | solution.py:331
  268.9 34.5 %collective-permute-start.21 = (bf16[4,512,768]{2,1,0:T(8,128)(2,1)}, bf16[4,512,768]{2,1,0:T(8,128)(2,1)}, u32[]{:S(2)}, u32[]{:S(2)}) collective-permute-start(bf16[4,512,768]{2,1,0:T(8,128)(2,1)} %up_give.1), channel_id=1, source_target_pairs={{0,16},{16,0},{32,48},{48,32},{64,80},{80,64},{96,112},{112,96},{1... | collective-permute-start | bytes 9437192 | tf_op jit(solution)/shard_map/ppermute | solution.py:331
  281.8 33.7 %collective-permute-start.18 = (bf16[128,4096]{1,0:T(8,128)(2,1)}, bf16[128,4096]{1,0:T(8,128)(2,1)}, u32[]{:S(2)}, u32[]{:S(2)}) collective-permute-start(bf16[128,4096]{1,0:T(8,128)(2,1)} %get-tuple-element.73), channel_id=1, source_target_pairs={{0,3},{1,0},{2,1},{3,2},{4,7},{5,4},{6,5},{7,6},{8,11},{9,8},{10,9... | collective-permute-start | bytes 3145736 | tf_op jit(solution)/shard_map/ppermute | solution.py:32
  281.8 35.5 %collective-permute-start.19 = (bf16[128,4096]{1,0:T(8,128)(2,1)}, bf16[128,4096]{1,0:T(8,128)(2,1)}, u32[]{:S(2)}, u32[]{:S(2)}) collective-permute-start(bf16[128,4096]{1,0:T(8,128)(2,1)} %get-tuple-element.74), channel_id=1, source_target_pairs={{0,1},{1,2},{2,3},{3,0},{4,5},{5,6},{6,7},{7,4},{8,9},{9,10},{10,1... | collective-permute-start | bytes 3145736 | tf_op jit(solution)/shard_map/ppermute | solution.py:32
  283.8 34.5 %collective-permute-start.20 = (bf16[128,4096]{1,0:T(8,128)(2,1)}, bf16[128,4096]{1,0:T(8,128)(2,1)}, u32[]{:S(2)}, u32[]{:S(2)}) collective-permute-start(bf16[128,4096]{1,0:T(8,128)(2,1)} %get-tuple-element.75), channel_id=1, source_target_pairs={{0,2},{1,3},{2,0},{3,1},{4,6},{5,7},{6,4},{7,5},{8,10},{9,11},{10,... | collective-permute-start | bytes 3145736 | tf_op jit(solution)/shard_map/ppermute | solution.py:32
  303.3 39.4 %collective-permute-start.27 = (bf16[96,4096]{1,0:T(8,128)(2,1)}, bf16[96,4096]{1,0:T(8,128)(2,1)S(1)}, u32[]{:S(2)}, u32[]{:S(2)}) collective-permute-start(bf16[96,4096]{1,0:T(8,128)(2,1)} %get-tuple-element.91), channel_id=1, source_target_pairs={{0,96},{16,112},{32,0},{48,16},{64,32},{80,48},{96,64},{112,80},{1... | collective-permute-start | bytes 2359304 | tf_op jit(solution)/shard_map/ppermute | solution.py:336
  315.4 27.3 %collective-permute-start.28 = (bf16[96,4096]{1,0:T(8,128)(2,1)S(1)}, bf16[96,4096]{1,0:T(8,128)(2,1)S(1)}, u32[]{:S(2)}, u32[]{:S(2)}) collective-permute-start(bf16[96,4096]{1,0:T(8,128)(2,1)S(1)} %copy-done.58), channel_id=1, source_target_pairs={{0,64},{16,80},{32,96},{48,112},{64,0},{80,16},{96,32},{112,48},{1... | collective-permute-start | bytes 2359304 | tf_op jit(solution)/shard_map/ppermute | solution.py:336
  317.3 40.4 %collective-permute-start.22 = (bf16[512,768]{1,0:T(8,128)(2,1)S(1)}, bf16[512,768]{1,0:T(8,128)(2,1)S(1)}, u32[]{:S(2)}, u32[]{:S(2)}) collective-permute-start(bf16[512,768]{1,0:T(8,128)(2,1)S(1)} %get-tuple-element.81), channel_id=1, source_target_pairs={{0,32},{16,48},{32,64},{48,80},{64,96},{80,112},{96,0},{112,16},{1... | collective-permute-start | bytes 2359304 | tf_op jit(solution)/shard_map/ppermute | solution.py:336
  318.3 55.7 %collective-permute-start.23 = (bf16[512,768]{1,0:T(8,128)(2,1)S(1)}, bf16[512,768]{1,0:T(8,128)(2,1)S(1)}, u32[]{:S(2)}, u32[]{:S(2)}) collective-permute-start(bf16[512,768]{1,0:T(8,128)(2,1)S(1)} %get-tuple-element.82), channel_id=1, source_target_pairs={{0,96},{16,112},{32,0},{48,16},{64,32},{80,48},{96,64},{112,80},{1... | collective-permute-start | bytes 2359304 | tf_op jit(solution)/shard_map/ppermute | solution.py:336
  324.0 51.8 %collective-permute-start.24 = (bf16[512,768]{1,0:T(8,128)(2,1)S(1)}, bf16[512,768]{1,0:T(8,128)(2,1)S(1)}, u32[]{:S(2)}, u32[]{:S(2)}) collective-permute-start(bf16[512,768]{1,0:T(8,128)(2,1)S(1)} %get-tuple-element.83), channel_id=1, source_target_pairs={{0,64},{16,80},{32,96},{48,112},{64,0},{80,16},{96,32},{112,48},{1... | collective-permute-start | bytes 2359304 | tf_op jit(solution)/shard_map/ppermute | solution.py:336
  (72 other events, 920.5 us)
